TPU v7x, 128 devices: a whole 4x4x4 slice. The times are simulated.
128 devices in a mesh: tiles: 32 (over z, y, core), members: 4 (over x).
Axes of the slice: x: 4, y: 4, z: 4, core: 2. Of those that a mesh axis runs over, the one named last changes fastest.
Arguments:
- features: bfloat16 [4, 96, 32, 32, 256], P('members', 'tiles'), may hold values from -6 to 6
- conv_one: bfloat16 [3, 3, 256, 256], replicated, may hold values from -0.125 to 0.125
- conv_two: bfloat16 [3, 3, 256, 256], replicated, may hold values from -0.125 to 0.125
- cotangent: bfloat16 [4, 96, 32, 32, 256], P('members', 'tiles'), may hold values from -6 to 6
- neighbour_tile: int32 [96, 4], P('tiles'), may hold values from 0 to 95, as said below
- rotation: int32 [96, 4], P('tiles'), may hold values from 0 to 7
Outputs:
- output: bfloat16 [4, 96, 32, 32, 256], P('members', 'tiles')
- grad_features: bfloat16 [4, 96, 32, 32, 256], P('members', 'tiles')
- grad_one: float32 [3, 3, 256, 256], replicated
- grad_two: float32 [3, 3, 256, 256], replicated
Inputs may be any that keep to these rules, and one draw needn't show every extreme that they name: neighbour_tile and rotation describe the tiles of the six faces of a cube, 16 of them on each face in a square: each tile edge borders exactly one edge of another tile, and the relation is symmetric: if t2 = neighbour_tile[t, e] and e2 = rotation[t, e] % 4 then neighbour_tile[t2, e2] = t and rotation[t2, e2] = e + 4 * (rotation[t, e] // 4).
All inputs are finite; a program needn't handle non-finite values.
Results may differ from a plain program's by a relative error of at most 0.0051.
Values may be sent and summed in bfloat16 or wider, within the bound.
A program may use at most 128 MiB of HBM per device.

v0:
```python
import math

import jax
import jax.numpy as jnp
from jax import lax
from jax.sharding import PartitionSpec as P


def edges_of(values):
    top_edge = values[:, 0]
    bottom_edge = values[:, -1]
    left_edge = values[:, :, 0]
    right_edge = values[:, :, -1]
    stacked = jnp.stack([top_edge, bottom_edge, left_edge, right_edge], axis=1)
    return stacked.reshape(-1, values.shape[2], values.shape[3])


def orient(seam_vals, rotation):
    flipped = (rotation // 4)[:, :, None, None] == 1
    return jnp.where(flipped, seam_vals[:, :, ::-1], seam_vals)


def seam_rows(edge_list, neighbour_tile, rotation):
    source = 4 * neighbour_tile + rotation % 4
    return orient(edge_list[source], rotation)


def pad_tiles(values, seam_vals):
    zero_col = jnp.zeros_like(seam_vals[:, 0, :1])
    top_row = jnp.concatenate([zero_col, seam_vals[:, 0], zero_col], axis=1)[:, None]
    bottom_row = jnp.concatenate([zero_col, seam_vals[:, 1], zero_col], axis=1)[:, None]
    middle = jnp.concatenate(
        [seam_vals[:, 2][:, :, None], values, seam_vals[:, 3][:, :, None]], axis=2
    )
    return jnp.concatenate([top_row, middle, bottom_row], axis=1)


def outer_rows(padded):
    return jnp.stack(
        [padded[:, 0, 1:-1], padded[:, -1, 1:-1], padded[:, 1:-1, 0], padded[:, 1:-1, -1]], axis=1
    )


def add_edges(interior, returned):
    interior = interior.at[:, 0].add(returned[:, 0])
    interior = interior.at[:, -1].add(returned[:, 1])
    interior = interior.at[:, :, 0].add(returned[:, 2])
    return interior.at[:, :, -1].add(returned[:, 3])


def convolve(padded, kernel):
    return lax.conv_general_dilated(
        padded,
        kernel,
        (1, 1),
        "VALID",
        dimension_numbers=("NHWC", "HWIO", "NHWC"),
        preferred_element_type=jnp.float32,
    )


def spread(gradient, kernel):
    turned = jnp.transpose(kernel[::-1, ::-1], (0, 1, 3, 2))
    return lax.conv_general_dilated(
        gradient,
        turned,
        (1, 1),
        ((2, 2), (2, 2)),
        dimension_numbers=("NHWC", "HWIO", "NHWC"),
        preferred_element_type=jnp.float32,
    )


def kernel_grad(padded, gradient):
    return lax.conv_general_dilated(
        padded,
        gradient,
        (1, 1),
        "VALID",
        dimension_numbers=("CHWN", "IHWO", "HWNC"),
        preferred_element_type=jnp.float32,
    )


def widen(values, neighbour_tile, rotation):
    edge_list = lax.all_gather(edges_of(values), "tiles", axis=0, tiled=True)
    seam_vals = seam_rows(edge_list, neighbour_tile, rotation)
    return pad_tiles(values, seam_vals)


def return_rims(spread_out, neighbour_tile, rotation):
    interior = spread_out[:, 1:-1, 1:-1]
    rim_vals = outer_rows(spread_out).astype(jnp.bfloat16)
    cells = rim_vals.shape[2]
    chans = rim_vals.shape[3]
    rim_list = lax.all_gather(rim_vals.reshape(-1, cells, chans), "tiles", axis=0, tiled=True)
    returned = seam_rows(rim_list, neighbour_tile, rotation).astype(jnp.float32)
    return add_edges(interior, returned)


def on_device(features, conv_one, conv_two, cotangent, neighbour_tile, rotation):
    values = features[0]
    grad_out = cotangent[0]
    tiles_here = values.shape[0]
    cells_all = (
        lax.axis_size("members")
        * lax.axis_size("tiles")
        * tiles_here
        * values.shape[1]
        * values.shape[2]
    )
    factor = 1.0 / math.sqrt(cells_all)
    padded_in = widen(values, neighbour_tile, rotation)
    preact = convolve(padded_in, conv_one)
    activation = jax.nn.silu(preact).astype(jnp.bfloat16)
    padded_act = widen(activation, neighbour_tile, rotation)
    output = convolve(padded_act, conv_two).astype(jnp.bfloat16)
    second = kernel_grad(padded_act, grad_out)
    d_act = return_rims(spread(grad_out, conv_two), neighbour_tile, rotation)
    sigmoid_v = jax.nn.sigmoid(preact)
    d_pre = (d_act * sigmoid_v * (1.0 + preact * (1.0 - sigmoid_v))).astype(jnp.bfloat16)
    first = kernel_grad(padded_in, d_pre)
    grad_in = return_rims(spread(d_pre, conv_one), neighbour_tile, rotation).astype(jnp.bfloat16)
    first, second = lax.psum((first, second), ("tiles", "members"))
    return (output[None], grad_in[None], first * factor, second * factor)


def solution(mesh):
    placed = (
        P("members", "tiles", None, None, None),
        P(),
        P(),
        P("members", "tiles", None, None, None),
        P("tiles", None),
        P("tiles", None),
    )
    return jax.shard_map(
        on_device,
        mesh=mesh,
        in_specs=placed,
        out_specs=(
            P("members", "tiles", None, None, None),
            P("members", "tiles", None, None, None),
            P(),
            P(),
        ),
        check_vma=False,
    )
```

profile of v0, /device:TPU:1, one launch (start us, length us, event | category | flops | bytes accessed | tf_op | source)
XLA Modules:
  0.0 433.8 jit_solution(7910245941253485943)
XLA Ops:
  7.2 2.9 copy.205
  10.2 1.5 copy.206
  12.0 0.7 copy.99
  12.8 2.3 copy.207
  15.7 0.9 copy-done.28
  16.7 9.5 %fusion.85 = (bf16[34,24,5,256]{3,1,2,0:T(8,128)(2,1)S(1)}, f32[34,24,5,256]{3,1,2,0:T(8,128)}) fusion(bf16[3,3,256,256]{3,2,1,0:T(8,128)(2,1)S(1)} %copy-done.28, bf16[32,3,8,7,256]{4,0,3,2,1:T(8,128)(2,1)S(1)} %fusion.25, pred[24,5]{0,1:T(8,128)(4,1)S(1)} %copy-done.31), kind=kOutput, calls=%fused_computation.156 | convolution fusion | flops 4531937280 | bytes 10199160 | tf_op jit(solution)/shard_map/conv_general_dilated | solution.py:64
  26.2 0.5 copy.125
  27.1 0.7 copy.128
  28.3 37.6 %all-gather.5.cloned.1.call-done = bf16[384,32,256]{2,1,0:T(8,128)(2,1)} async-done(((bf16[12,32,256]{2,1,0:T(8,128)(2,1)}), bf16[384,32,256]{2,1,0:T(8,128)(2,1)}) %all-gather.5.cloned.1.call-update) | async-done | bytes 6291472 | tf_op jit(solution)/shard_map/all_gather | solution.py:86
  65.8 4.0 gather_fusion
  69.9 1.1 copy.100
  71.0 45.9 %all-gather.9.cloned.1.call-done = bf16[384,32,256]{2,1,0:T(8,128)(2,1)} async-done(((bf16[12,32,256]{2,1,0:T(8,128)(2,1)}), bf16[384,32,256]{2,1,0:T(8,128)(2,1)}) %all-gather.9.cloned.1.call-update) | async-done | bytes 6291472 | tf_op jit(solution)/shard_map/all_gather | solution.py:96
  116.8 4.0 gather_fusion.2
  120.8 1.1 copy.129
  121.9 1.2 fusion.45
  123.4 0.5 copy-done.16
  123.9 2.1 fusion.79
  126.0 1.4 pad.16
  127.4 0.6 copy.105
  128.2 7.7 %add_divide_fusion = (f32[32,24,5,256]{3,1,2,0:T(8,128)}, bf16[32,24,5,256]{3,1,2,0:T(8,128)(2,1)S(1)}, f32[32,24,5,256]{3,1,2,0:T(8,128)}) fusion(pred[24,5]{0,1:T(8,128)(4,1)S(1)} %copy-done.29, bf16[3,3,256,256]{3,2,1,0:T(8,128)(2,1)S(1)} %copy-done, bf16[34,3,7,2,256]{4,2,1,3,0:T(8,128)(2,1)S(1)} %slice.402, bf16[34,3,8,5,256]{4,2,1,3,0:T(8,128)(2,1)S(1)} %copy.105), kind=kOutput, calls=%fused_computation.21 | convolution fusion | flops 4547469312 | bytes 13830264 | tf_op jit(solution)/shard_map/conv_general_dilated | solution.py:52
  136.0 0.6 fusion.84
  137.1 1.3 slice.407
  138.4 0.7 reshape.330
  139.0 0.8 copy.108
  139.9 0.7 reshape.332
  140.5 2.8 copy.204
  143.3 1.3 copy-done.5
  145.0 0.7 copy.113
  146.0 3.6 copy.123
  150.0 2.4 copy.203
  152.4 1.1 slice.418
  153.6 1.0 copy-done.11
  154.6 1.3 copy.133
  156.3 1.7 copy-done.10
  158.0 1.3 copy.135
  159.6 0.7 copy-done.13
  160.5 8.4 %fusion.5 = bf16[3,32,32,256]{3,0,1,2:T(4,128)(2,1)S(1)} fusion(f32[32,3,32,256]{3,0,2,1:T(8,128)S(1)} %slice.433, f32[3,32,32,256]{3,0,1,2:T(4,128)S(1)} %fusion.56, f32[32,3,32,256]{3,0,2,1:T(8,128)S(1)} %slice.432), kind=kLoop, calls=%fused_computation.15 | loop fusion | flops 2359296 | bytes 11010048 | tf_op jit(solution)/shard_map/convert_element_type | solution.py:121
  169.0 1.2 pad.22
  170.2 2.1 copy.138
  172.5 6.7 %fusion.86 = (bf16[34,24,5,256]{3,1,2,0:T(8,128)(2,1)S(1)}, f32[34,24,5,256]{3,1,2,0:T(8,128)}) fusion(bf16[3,3,256,256]{3,2,1,0:T(8,128)(2,1)S(1)} %copy-done, bf16[32,3,7,2,256]{4,2,1,3,0:T(8,128)(2,1)S(1)} %slice.434, bf16[32,3,8,5,256]{4,2,1,3,0:T(8,128)(2,1)S(1)} %copy.138, pred[24,5]{0,1:T(8,128)(4,1)S(1)} %copy-done.31), kind=kOutput, calls=%fused_computation.157 | convolution fusion | flops 4540194816 | bytes 10100856 | tf_op jit(solution)/shard_map/conv_general_dilated | solution.py:64
  180.2 0.7 copy.144
  181.1 13.4 %fusion.34 = f32[3,3,256,256]{3,2,1,0:T(8,128)} fusion(bf16[3,32,32,256]{3,0,1,2:T(4,128)(2,1)} %copy-done.8, bf16[3,1,34,256]{3,0,2,1:T(4,128)(2,1)S(1)} %get-tuple-element.142, bf16[3,32,1,256]{3,0,2,1:T(4,128)(2,1)S(1)} %copy-done.17, bf16[3,32,32,256]{3,0,2,1:T(4,128)(2,1)S(1)} %bitcast.215, bf16[3,32,1,256]{3,0,2,1:T(4,128)(2,1)S(1)} %copy-done.19, ...), kind=kOutput, calls=%fused_computation.50 | convolution fusion | flops 3632756736 | bytes 5707776 | tf_op jit(solution)/shard_map/conv_general_dilated | solution.py:75
  194.5 3.6 copy.139
  198.4 2.8 copy.202
  201.2 2.1 copy-done.3
  203.3 3.3 slice.436
  206.6 3.5 gather_fusion.1
  210.3 34.6 %all-gather.11.cloned.1.call-done = bf16[384,32,256]{2,1,0:T(8,128)(2,1)} async-done(((bf16[12,32,256]{2,1,0:T(8,128)(2,1)}), bf16[384,32,256]{2,1,0:T(8,128)(2,1)}) %all-gather.11.cloned.1.call-update) | async-done | bytes 6291472 | tf_op jit(solution)/shard_map/all_gather | solution.py:96
  244.9 3.3 gather_fusion.3
  248.4 1.2 fusion.46
  249.8 3.2 fusion.80
  253.0 12.5 %fusion.32 = f32[3,3,256,256]{3,2,1,0:T(8,128)} fusion(bf16[3,32,32,256]{3,2,1,0:T(8,128)(2,1)S(1)} %bitcast.226, bf16[3,1,34,256]{3,0,2,1:T(4,128)(2,1)S(1)} %get-tuple-element.140, bf16[3,32,1,256]{3,0,2,1:T(4,128)(2,1)S(1)} %get-tuple-element.133, bf16[3,32,32,256]{3,0,2,1:T(4,128)(2,1)S(1)} %bitcast.218, ...), kind=kOutput, calls=%fused_computation.47 | convolution fusion | flops 3632756736 | bytes 5707776 | tf_op jit(solution)/shard_map/conv_general_dilated | solution.py:75
  265.6 1.4 pad.18
  267.0 0.6 copy.119
  267.8 0.6 copy-done.30
  268.5 6.3 %select_convert_fusion = bf16[32,24,5,256]{3,1,2,0:T(8,128)(2,1)S(1)} fusion(pred[24,5]{0,1:T(8,128)(4,1)S(1)} %copy-done.30, bf16[3,3,256,256]{3,2,1,0:T(8,128)(2,1)} %param.24, bf16[34,3,7,2,256]{4,2,1,3,0:T(8,128)(2,1)S(1)} %slice.414, bf16[34,3,8,5,256]{4,2,1,3,0:T(8,128)(2,1)S(1)} %copy.119), kind=kOutput, calls=%fused_computation.18 | convolution fusion | flops 4540588032 | bytes 5965944 | tf_op jit(solution)/shard_map/conv_general_dilated | solution.py:52
  275.3 2.0 copy.151
  277.4 0.6 copy-done.2
  278.1 1.0 fusion.54
  279.2 0.9 convert_bitcast_fusion
  280.1 2.3 copy.152
  282.4 139.6 %all-reduce.3.cloned.1.call-done = (f32[3,3,256,256]{3,2,1,0:T(8,128)}, f32[3,3,256,256]{3,2,1,0:T(8,128)}) async-done(((f32[3,3,256,256]{3,2,1,0:T(8,128)}, f32[3,3,256,256]{3,2,1,0:T(8,128)}), (f32[3,3,256,256]{3,2,1,0:T(8,128)}, f32[3,3,256,256]{3,2,1,0:T(8,128)})) %all-reduce.3.cloned.1.call-update) | async-done | bytes 4718608 | tf_op jit(solution)/shard_map/psum | solution.py:124
  422.0 3.4 broadcast_multiply_fusion.1
  425.4 1.6 broadcast_multiply_fusion
  (123 shorter events, 8.0 us)
Async XLA Ops:
  7.2 121.0 %copy-start = (bf16[3,3,256,256]{3,2,1,0:T(8,128)(2,1)S(1)}, bf16[3,3,256,256]{3,2,1,0:T(8,128)(2,1)}, u32[]{:S(2)}) copy-start(bf16[3,3,256,256]{3,2,1,0:T(8,128)(2,1)} %param.23) | copy-start | bytes 3538948
  7.2 58.7 %all-gather.5.cloned.1.call-start = ((), (), s32[]{:S(2)}) async-start(), calls=%async_computation | async-start | bytes 6488064 | tf_op jit(solution)/shard_map/all_gather | solution.py:86
  7.2 2.9 copy-start.9
  12.7 104.1 %all-gather.9.cloned.1.call-start = ((), (), s32[]{:S(2)}) async-start(), calls=%async_computation.2 | async-start | bytes 6488064 | tf_op jit(solution)/shard_map/all_gather | solution.py:96
  15.4 1.3 copy-start.28
  15.4 1.3 copy-start.31
  26.6 1.4 copy-start.24
  26.6 1.5 copy-start.27
  27.8 178.8 %all-gather.7.cloned.1.call-start = ((), (), s32[]{:S(2)}) async-start(), calls=%async_computation.1 | async-start | bytes 6488064 | tf_op jit(solution)/shard_map/all_gather | solution.py:86
  28.1 97.8 %copy-start.25 = (pred[3,4]{0,1:T(4,128)(4,1)}, pred[3,4]{0,1:T(4,128)(4,1)S(1)}, u32[]{:S(2)}) copy-start(pred[3,4]{0,1:T(4,128)(4,1)S(1)} %copy.96) | copy-start | bytes 40
  28.3 97.7 %copy-start.20 = (s32[1024]{0:T(1024)}, s32[1024]{0:T(1024)S(1)}, u32[]{:S(2)}) copy-start(s32[1024]{0:T(1024)S(1)} %pad_clamp_fusion) | copy-start | bytes 12292
  123.2 0.6 copy-start.16
  123.2 0.6 copy-start.18
  123.2 4.2 copy-start.22
  127.4 0.8 copy-start.29
  140.5 4.1 slice-start
  140.5 4.2 slice-start.1
  143.3 1.3 copy-start.5
  145.8 99.1 %all-gather.11.cloned.1.call-start = ((), (), s32[]{:S(2)}) async-start(), calls=%async_computation.3 | async-start | bytes 6488064 | tf_op jit(solution)/shard_map/all_gather | solution.py:96
  152.4 2.2 copy-start.11
  155.9 2.1 copy-start.10
  159.2 1.1 copy-start.13
  169.0 3.3 copy-start.8
  179.7 1.4 copy-start.17
  179.7 1.4 copy-start.19
  180.9 241.1 %all-reduce.3.cloned.1.call-start = ((), (), s32[]{:S(2)}) async-start(), calls=%async_computation.4 | async-start | bytes 9437184 | tf_op jit(solution)/shard_map/psum | solution.py:124
  201.2 2.1 copy-start.3
  203.3 3.3 copy-start.21
  203.3 45.1 %copy-start.26 = (pred[3,4]{0,1:T(4,128)(4,1)S(1)}, pred[3,4]{0,1:T(4,128)(4,1)}, u32[]{:S(2)}) copy-start(pred[3,4]{0,1:T(4,128)(4,1)} %copy-done.25) | copy-start | bytes 40
  206.6 43.1 %copy-start.23 = (bf16[3,1,256]{2,0,1:T(4,128)(2,1)S(1)}, bf16[3,1,256]{2,0,1:T(4,128)(2,1)}, u32[]{:S(2)}) copy-start(bf16[3,1,256]{2,0,1:T(4,128)(2,1)} %copy-done.22) | copy-start | bytes 4612
  206.6 43.2 %copy-start.6 = (bf16[32,3,32,256]{3,1,2,0:T(4,128)(2,1)S(1)}, bf16[32,3,32,256]{3,1,2,0:T(4,128)(2,1)}, u32[]{:S(2)}) copy-start(bf16[32,3,32,256]{3,1,2,0:T(4,128)(2,1)} %copy-done.5) | copy-start | bytes 4718596
  249.6 3.4 copy-start.7
  249.6 3.4 copy-start.15
  253.0 12.5 %copy-start.4 = (bf16[34,3,34,256]{3,1,2,0:T(4,128)(2,1)S(1)}, bf16[34,3,34,256]{3,1,2,0:T(4,128)(2,1)}, u32[]{:S(2)}) copy-start(bf16[34,3,34,256]{3,1,2,0:T(4,128)(2,1)} %fusion.80) | copy-start | bytes 5326852
  267.8 0.7 copy-start.30
  275.2 2.8 copy-start.2
  275.2 2.9 copy-start.14
  422.0 3.4 copy-start.12
  422.0 5.0 %copy-start.1 = (bf16[3,3,256,256]{3,2,1,0:T(8,128)(2,1)S(1)}, bf16[3,3,256,256]{3,2,1,0:T(8,128)(2,1)}, u32[]{:S(2)}) copy-start(bf16[3,3,256,256]{3,2,1,0:T(8,128)(2,1)} %param.23) | copy-start | bytes 3538948
Sparse Core Ops, SparseCore 0:
  12.9 52.9 all-gather.4
  68.7 48.1 all-gather.8
  145.9 48.1 all-gather.6
  196.7 48.1 all-gather.10
  267.9 154.0 all-reduce.2
where the time goes:
time: 442 us; the launch traced here: 434 us
  waiting for transfers between devices  258 us (58%)
  local copies, waits for them, and re-layouts  80 us (18%)
  matrix products  56.1 us (13%)
  other arithmetic  24.4 us (6%)
  between operations  14.8 us (3%)
    psum x1, waiting for transfers between devices, on_device(): first, second = lax.psum((first, second), ('tiles', 'members'))  140 us
    all_gather x2, waiting for transfers between devices, return_rims(): lax.all_gather(rim_vals.reshape(-1, cells, chans), 'tiles', axis=0, tiled...  80.5 us
    all_gather x2, waiting for transfers between devices, widen(): edge_list = lax.all_gather(edges_of(values), 'tiles', axis=0, tiled=True)  37.6 us
    conv_general_dilated x2, matrix products, kernel_grad(): lax.conv_general_dilated(padded, gradient, (1, 1), 'VALID', dimension_num...  25.9 us
    unnamed x75, local copies, waits for them, and re-layouts  25.9 us
    gather x8, local copies, waits for them, and re-layouts, seam_rows(): return orient(edge_list[source], rotation)  17.4 us
    conv_general_dilated x2, matrix products, spread(): lax.conv_general_dilated(gradient, turned, (1, 1), ((2, 2), (2, 2)), dime...  16.2 us
    conv_general_dilated x2, matrix products, convolve(): lax.conv_general_dilated(padded, kernel, (1, 1), 'VALID', dimension_numbe...  14 us
  transfers between devices with their start and end apart: 5, of which 4 were waited for; matrix products, arithmetic and copies ran while one was open for 21% of the time, Pallas kernels for 0%

commit v1 on v0

v1 whole, which is shorter than its diff:
```python
import functools
import math

import jax
import jax.numpy as jnp
from jax import lax
from jax.experimental import pallas as pl
from jax.experimental.pallas import tpu as pltpu
from jax.sharding import PartitionSpec as P

MESH = pl.DeviceIdType.MESH
F32 = jnp.float32
BF16 = jnp.bfloat16
ROWS = 512


def kernel(
    feat, cot, w1, w2, tab, loc,
    out, gfeat, full1, full2,
    fa3, c3, d3, wt, pre, dact, xt, grad, seams, edges, mats,
    edge_out, ag0, ag1, ag2, ag3, pick, got0, got1, got2, got3, tabv, tabs,
    corr, snd, rcore, sx, rx, sy, ry, sz, rz,
    tab_s, tab_r, ag_s, ag_r, pk_s, pk_r, ar_s, ar_r, loc_sem,
):
    ag = (ag0, ag1, ag2, ag3)
    got = (got0, got1, got2, got3)
    me = lax.axis_index("tiles")
    xpos = lax.axis_index("members")
    core = lax.rem(me, 2)
    ypos = lax.rem(me // 2, 4)
    zpos = me // 8
    ring = zpos * (1 - core) + ypos * core
    other = ypos * (1 - core) + zpos * core

    def tid(z, y, c):
        return (z * 4 + y) * 2 + c

    partner = tid(zpos, ypos, 1 - core)

    def wrap(v):
        return lax.rem(v, 4)

    barrier = pltpu.get_barrier_semaphore()
    pl.semaphore_signal(barrier, inc=1, device_id={"tiles": partner}, device_id_type=MESH)
    for d in range(1, 4):
        for c in range(2):
            pl.semaphore_signal(barrier, inc=1, device_id={"tiles": tid(wrap(zpos + d), ypos, c)}, device_id_type=MESH)
            pl.semaphore_signal(barrier, inc=1, device_id={"tiles": tid(zpos, wrap(ypos + d), c)}, device_id_type=MESH)
        pl.semaphore_signal(barrier, inc=1, device_id={"members": wrap(xpos + d)}, device_id_type=MESH)
    pl.semaphore_wait(barrier, 16)

    def remote(src, dst, ssem, rsem, target):
        return pltpu.make_async_remote_copy(
            src_ref=src, dst_ref=dst, send_sem=ssem, recv_sem=rsem,
            device_id={"tiles": target}, device_id_type=MESH,
        )

    def remote_x(src, dst, ssem, rsem, target):
        return pltpu.make_async_remote_copy(
            src_ref=src, dst_ref=dst, send_sem=ssem, recv_sem=rsem,
            device_id={"members": target}, device_id_type=MESH,
        )

    tab_copies = []
    for d in range(1, 4):
        tab_copies.append(remote(tab.at[0], tabv.at[ypos * 2 + core], tab_s.at[d - 1], tab_r.at[ypos * 2 + core], tid(zpos, wrap(ypos + d), 0)))
        tab_copies.append(remote(tab.at[1], tabv.at[zpos * 2 + core], tab_s.at[d + 2], tab_r.at[zpos * 2 + core], tid(wrap(zpos + d), ypos, 1)))
    slot_p = (ypos * core + zpos * (1 - core)) * 2 + core
    tab_copies.append(remote(tab.at[1 - core], tabv.at[slot_p], tab_s.at[6], tab_r.at[slot_p], partner))
    for copy in tab_copies:
        copy.start()
    tab_own = pltpu.make_async_copy(tab.at[core], tabv.at[other * 2 + core], loc_sem.at[0])
    tab_own.start()

    r_i = lax.broadcasted_iota(jnp.int32, (128, 1024), 0)
    c_i = lax.broadcasted_iota(jnp.int32, (128, 1024), 1)
    e_i = r_i // 32
    k_i = r_i - e_i * 32
    want = jnp.where(e_i == 0, k_i, jnp.where(e_i == 1, 992 + k_i, jnp.where(e_i == 2, 32 * k_i, 32 * k_i + 31)))
    pickrow = jnp.where(c_i == want, 1.0, 0.0).astype(BF16)
    m_r = lax.broadcasted_iota(jnp.int32, (96, 32), 0)
    m_c = lax.broadcasted_iota(jnp.int32, (96, 32), 1)
    m_b = m_r // 32
    m_t = m_r - m_b * 32 + m_b - 1
    mats[0] = jnp.where(m_c == m_t, 1.0, 0.0).astype(BF16)
    mats[1] = jnp.where((31 - m_c == m_t), 1.0, 0.0).astype(BF16)

    def dot(a, b):
        return jnp.dot(a, b, preferred_element_type=F32)

    def dot_nt(a, b):
        return lax.dot_general(a, b, (((1,), (1,)), ((), ())), preferred_element_type=F32)

    def dot_tn(a, b):
        return lax.dot_general(a, b, (((0,), (0,)), ((), ())), preferred_element_type=F32)

    def take_edges(get, which):
        for t in range(3):
            picked = dot(pickrow, get(t)).astype(BF16)
            for e in range(4):
                edges[which, e, t * 32:t * 32 + 32, :] = picked[e * 32:e * 32 + 32]

    def put_edge(n, t, e, value):
        edge_out[n, 0, t * 4 + e] = value[:, 0:128]
        edge_out[n, 1, t * 4 + e] = value[:, 128:256]

    def send_edges(n):
        copies = []
        for d in range(1, 4):
            copies.append(remote(edge_out.at[n, 0], ag[n].at[pl.ds((zpos * 2 + core) * 12, 12)], ag_s.at[n, d - 1], ag_r.at[n, zpos * 2 + core], tid(wrap(zpos + d), ypos, 0)))
            copies.append(remote(edge_out.at[n, 1], ag[n].at[pl.ds((ypos * 2 + core) * 12, 12)], ag_s.at[n, d + 2], ag_r.at[n, ypos * 2 + core], tid(zpos, wrap(ypos + d), 1)))
        slot = (zpos * core + ypos * (1 - core)) * 2 + core
        copies.append(remote(edge_out.at[n, 1 - core], ag[n].at[pl.ds((slot) * 12, 12)], ag_s.at[n, 6], ag_r.at[n, slot], partner))
        for copy in copies:
            copy.start()
        own = pltpu.make_async_copy(edge_out.at[n, core], ag[n].at[pl.ds((ring * 2 + core) * 12, 12)], loc_sem.at[1])
        own.start()
        own.wait()
        return copies

    def forward(n):
        for d in range(1, 4):
            for c in range(2):
                slot = wrap(ring + d) * 2 + c
                remote(edge_out.at[n, 0], ag[n].at[pl.ds((slot) * 12, 12)], ag_s.at[n, 0], ag_r.at[n, slot], partner).wait_recv()
        slot = ring * 2 + 1 - core
        remote(edge_out.at[n, 0], ag[n].at[pl.ds((slot) * 12, 12)], ag_s.at[n, 0], ag_r.at[n, slot], partner).wait_recv()

        def choose(q, carry):
            for k in range(12):
                pick[n, q, k] = ag[n][tabs[q, 0, k]]
            return carry

        lax.fori_loop(0, 8, choose, 0)
        copies = []
        for d in range(1, 4):
            p = wrap(other + d)
            for c in range(2):
                target = tid(zpos * (1 - core) + p * core, p * (1 - core) + ypos * core, c)
                copies.append(remote(pick.at[n, p * 2 + c], got[n].at[core, other], pk_s.at[n, d * 2 + c - 2], pk_r.at[n, core * 4 + other], target))
        copies.append(remote(pick.at[n, other * 2 + 1 - core], got[n].at[core, other], pk_s.at[n, 6], pk_r.at[n, core * 4 + other], partner))
        for copy in copies:
            copy.start()
        own = pltpu.make_async_copy(pick.at[n, other * 2 + core], got[n].at[core, other], loc_sem.at[2])
        own.start()
        own.wait()
        return copies

    def arrive(n):
        def wait(h, p):
            remote(pick.at[n, 0], got[n].at[h, p], pk_s.at[n, 0], pk_r.at[n, h * 4 + p], partner).wait_recv()

        for d in range(1, 4):
            wait(0, wrap(ypos + d))
            wait(1, wrap(zpos + d))
        wait(1 - core, zpos * (1 - core) + ypos * core)

    def received(n, k):
        left = got[n][0, loc[0, k], k]
        right = got[n][1, loc[1, k], k]
        return jnp.concatenate([left, right], axis=1)

    def take_seams(n):
        for t in range(3):
            for e in range(4):
                k = t * 4 + e
                both = dot(mats[loc[2, k]], received(n, k)).astype(BF16)
                for b in range(3):
                    seams[e, t * 32:t * 32 + 32, b * 256:b * 256 + 256] = both[b * 32:b * 32 + 32]

    jj = lax.rem(lax.broadcasted_iota(jnp.int32, (128, 256), 0), 32)

    def put3(dst, t, r, x):
        row = pl.multiple_of(32 + r * 128, 32)
        dst[t, pl.ds(row, 128), 256:512] = x.astype(BF16)
        dst[t, pl.ds(row, 128), 0:256] = jnp.where(jj == 0, 0.0, pltpu.roll(x, 1, 0)).astype(BF16)
        dst[t, pl.ds(row, 128), 512:768] = jnp.where(jj == 31, 0.0, pltpu.roll(x, 127, 0)).astype(BF16)

    def each_chunk(body):
        def step(i, carry):
            t = i // 8
            body(t, i - t * 8)
            return carry

        lax.fori_loop(0, 24, step, 0)

    def conv3(x3, weight, store):
        parts = 1024 // ROWS

        def step(i, carry):
            t = i // parts
            r = (i - t * parts) * ROWS
            acc = dot(x3[t, pl.ds(pl.multiple_of(r, 32), ROWS), :], weight(0))
            acc = acc + dot(x3[t, pl.ds(pl.multiple_of(r + 32, 32), ROWS), :], weight(1))
            acc = acc + dot(x3[t, pl.ds(pl.multiple_of(r + 64, 32), ROWS), :], weight(2))
            store(t, pl.multiple_of(r, 128), acc)
            return carry

        lax.fori_loop(0, 3 * parts, step, 0)

    def edge_weight(w, e):
        return [w[0, 0], w[0, 1], w[0, 2]] if e == 0 else [w[2, 0], w[2, 1], w[2, 2]] if e == 1 else [w[0, 0], w[1, 0], w[2, 0]] if e == 2 else [w[0, 2], w[1, 2], w[2, 2]]

    eight = lax.broadcasted_iota(jnp.int32, (8, 256), 0)

    def add_edge(dst, t, e, value_of):
        if e < 2:
            row = 0 if e == 0 else 992
            dst[t, row:row + 32, :] += value_of[t * 32:t * 32 + 32, :]
        else:
            base = 0 if e == 2 else 24
            at = 0 if e == 2 else 7

            def step(i, carry):
                row = pl.multiple_of(i * 32 + base, 8)
                line = value_of[pl.ds(t * 32 + i, 1), :]
                dst[t, pl.ds(row, 8), :] += jnp.where(eight == at, jnp.broadcast_to(line, (8, 256)), 0.0)
                return carry

            lax.fori_loop(0, 32, step, 0)

    def seam_conv(w, dst, corr):
        for e in range(4):
            ws = edge_weight(w, e)
            corr[...] = dot(seams[e, :, 0:256], ws[0]) + dot(seams[e, :, 256:512], ws[1]) + dot(seams[e, :, 512:768], ws[2])
            for t in range(3):
                add_edge(dst, t, e, corr)

    def rim_add(n, dst, corr):
        for e in range(4):
            for t in range(3):
                k = t * 4 + e
                corr[t * 32:t * 32 + 32, :] = dot(mats[loc[2, k], 32:64, :], received(n, k))
            for t in range(3):
                add_edge(dst, t, e, corr)

    def rims(which, w, n):
        for e in range(4):
            ws = edge_weight(w, e)
            for t in range(3):
                row = edges[which, e, t * 32:t * 32 + 32, :]
                three = dot(mats[0], row).astype(BF16)
                value = dot_nt(three[64:96], ws[0]) + dot_nt(three[32:64], ws[1]) + dot_nt(three[0:32], ws[2])
                put_edge(n, t, e, value.astype(BF16))

    def transpose_tile(x3, t):
        eye = jnp.where(lax.broadcasted_iota(jnp.int32, (256, 256), 0) == lax.broadcasted_iota(jnp.int32, (256, 256), 1), 1.0, 0.0).astype(BF16)
        xt[t] = dot_nt(eye, x3[t, 32:1056, 256:512]).astype(BF16)

    def turn_weight(w):
        for a in range(3):
            for b in range(3):
                wt[a, b * 256:b * 256 + 256, :] = w[2 - a, 2 - b].T

    def put_grad(a, b, value, first):
        for h in range(2):
            block = value[:, h * 128:h * 128 + 128].reshape(4, 4, 16, 128)
            if first:
                grad[h, :, :, a * 3 + b] = block
            else:
                grad[h, :, :, a * 3 + b] += block

    def grad_inner(g3):
        for t in range(3):
            for al in range(3):
                def step(be, carry):
                    value = dot(xt[t], g3[t, al * 32:al * 32 + 1024, pl.ds(pl.multiple_of(be * 256, 256), 256)])
                    ab = (2 - al) * 3 + 2 - be
                    for h in range(2):
                        block = value[:, h * 128:h * 128 + 128].reshape(4, 4, 16, 128)
                        if t == 0:
                            grad[h, :, :, ab] = block
                        else:
                            grad[h, :, :, ab] += block
                    return carry

                lax.fori_loop(0, 3, step, 0)

    def grad_seams(which):
        for e in range(4):
            for b in range(3):
                value = dot_tn(seams[e, :, b * 256:b * 256 + 256], edges[which, e])
                a, bb = [(0, b), (2, b), (b, 0), (b, 2)][e]
                put_grad(a, bb, value, False)

    def reduce_start(g):
        def step(i, carry):
            h = i // 4
            v = i - h * 4
            snd[g, h, v] = grad[h, v].astype(BF16)
            return carry

        lax.fori_loop(0, 8, step, 0)
        copy = remote(snd.at[g, 1 - core], rcore.at[g], ar_s.at[g, 0], ar_r.at[g, 0], partner)
        copy.start()
        return copy

    def reduce_finish(g, first, full):
        first.wait_recv()

        def add_core(i, carry):
            sx[g, i] = (grad[core, i] + rcore[g, i].astype(F32)).astype(BF16)
            return carry

        lax.fori_loop(0, 4, add_core, 0)
        sends = [first]

        def swap(src_of, dst_of, base, mine, send, target_of):
            cs = []
            for d in range(1, 4):
                p = wrap(mine + d)
                cs.append(send(src_of(p), dst_of(mine), ar_s.at[g, base + d - 1], ar_r.at[g, base + mine], target_of(p)))
            for c in cs:
                c.start()
            for d in range(1, 4):
                p = wrap(mine + d)
                send(src_of(p), dst_of(p), ar_s.at[g, base], ar_r.at[g, base + p], target_of(p)).wait_recv()
            sends.extend(cs)

        to_x = lambda p: p
        to_y = lambda p: tid(zpos, p, core)
        to_z = lambda p: tid(p, ypos, core)
        swap(lambda p: sx.at[g, p], lambda p: rx.at[g, p], 1, xpos, remote_x, to_x)
        total = sx[g, xpos].astype(F32)
        for d in range(1, 4):
            total = total + rx[g, wrap(xpos + d)].astype(F32)
        sy[g] = total.astype(BF16)
        swap(lambda p: sy.at[g, p], lambda p: ry.at[g, p], 5, ypos, remote, to_y)
        total = sy[g, ypos].astype(F32)
        for d in range(1, 4):
            total = total + ry[g, wrap(ypos + d)].astype(F32)
        sz[g] = total.astype(BF16)
        swap(lambda p: sz.at[g], lambda p: rz.at[g, p], 9, zpos, remote, to_z)
        rz[g, zpos] = sz[g]
        total = rz[g, 0].astype(F32) + rz[g, 1].astype(F32) + rz[g, 2].astype(F32) + rz[g, 3].astype(F32)
        full[core, xpos, ypos] = total.astype(BF16)
        swap(lambda p: full.at[core, xpos, ypos], lambda p: full.at[core, xpos, p], 13, ypos, remote, to_y)
        swap(lambda p: full.at[core, xpos], lambda p: full.at[core, p], 17, xpos, remote_x, to_x)
        last = remote(full.at[core], full.at[core], ar_s.at[g, 21], ar_r.at[g, 21], partner)
        last.start()
        remote(full.at[1 - core], full.at[1 - core], ar_s.at[g, 21], ar_r.at[g, 21], partner).wait_recv()
        sends.append(last)
        return sends

    sends = []
    take_edges(lambda t: feat[t].reshape(1024, 256), 0)
    for t in range(3):
        for e in range(4):
            put_edge(0, t, e, edges[0, e, t * 32:t * 32 + 32, :])
    sends += send_edges(0)
    take_edges(lambda t: cot[t].reshape(1024, 256), 1)
    rims(1, w2, 1)
    sends += send_edges(1)

    for x3 in (fa3, c3, d3):
        x3[:, 0:32, :] = jnp.zeros((3, 32, 768), BF16)
        x3[:, 1056:1088, :] = jnp.zeros((3, 32, 768), BF16)

    def load_feat(t, r):
        put3(fa3, t, r, feat[t, pl.ds(r * 4, 4)].reshape(128, 256).astype(F32))

    def load_cot(t, r):
        put3(c3, t, r, cot[t, pl.ds(r * 4, 4)].reshape(128, 256).astype(F32))

    each_chunk(load_feat)
    for d in range(1, 4):
        for c in range(2):
            slot = wrap(other + d) * 2 + c
            remote(tab.at[0], tabv.at[slot], tab_s.at[0], tab_r.at[slot], partner).wait_recv()
    slot = other * 2 + 1 - core
    remote(tab.at[0], tabv.at[slot], tab_s.at[0], tab_r.at[slot], partner).wait_recv()
    tab_own.wait()
    to_smem = pltpu.make_async_copy(tabv, tabs, loc_sem.at[3])
    to_smem.start()
    to_smem.wait()

    def store_pre(t, r, acc):
        pre[t, pl.ds(r, ROWS), :] = acc

    def store_dact(t, r, acc):
        dact[t, pl.ds(r, ROWS), :] = acc

    conv3(fa3, lambda a: w1[a].reshape(768, 256), store_pre)
    sends += forward(0)
    each_chunk(load_cot)
    turn_weight(w2)
    conv3(c3, lambda a: wt[a], store_dact)
    sends += forward(1)
    for t in range(3):
        transpose_tile(fa3, t)
    turn_weight(w1)

    arrive(0)
    take_seams(0)
    seam_conv(w1, pre, corr)
    arrive(1)
    rim_add(1, dact, corr)

    def nonlinear(t, r):
        row = pl.multiple_of(r * 128, 128)
        u = pre[t, pl.ds(row, 128), :]
        s = 1.0 / (1.0 + jnp.exp(-u))
        put3(fa3, t, r, (u * s).astype(BF16).astype(F32))
        d = dact[t, pl.ds(row, 128), :] * s * (1.0 + u * (1.0 - s))
        put3(d3, t, r, d.astype(BF16).astype(F32))

    each_chunk(nonlinear)

    take_edges(lambda t: fa3[t, 32:1056, 256:512], 2)
    for t in range(3):
        for e in range(4):
            put_edge(2, t, e, edges[2, e, t * 32:t * 32 + 32, :])
    sends += send_edges(2)
    take_edges(lambda t: d3[t, 32:1056, 256:512], 0)
    rims(0, w1, 3)
    sends += send_edges(3)
    grad_inner(d3)
    grad_seams(0)
    first1 = reduce_start(0)
    sends += forward(2)
    sends += reduce_finish(0, first1, full1)
    for t in range(3):
        transpose_tile(fa3, t)
    conv3(fa3, lambda a: w2[a].reshape(768, 256), store_pre)
    sends += forward(3)
    conv3(d3, lambda a: wt[a], store_dact)
    grad_inner(c3)
    arrive(2)
    take_seams(2)
    grad_seams(1)
    first2 = reduce_start(1)
    seam_conv(w2, pre, corr)
    arrive(3)
    rim_add(3, dact, corr)

    def finish(t, r):
        row = pl.multiple_of(r * 128, 128)
        out[t, pl.ds(row, 128), :] = pre[t, pl.ds(row, 128), :].astype(BF16)
        gfeat[t, pl.ds(row, 128), :] = dact[t, pl.ds(row, 128), :].astype(BF16)

    each_chunk(finish)
    sends += reduce_finish(1, first2, full2)
    for copy in sends + tab_copies:
        copy.wait_send()


def on_device(features, conv_one, conv_two, cotangent, neighbour_tile, rotation):
    cells_all = lax.axis_size("members") * lax.axis_size("tiles") * 3 * 1024
    factor = 1.0 / math.sqrt(cells_all)
    source = (4 * neighbour_tile + rotation % 4).reshape(12)
    device = source // 12
    z_of, y_of, c_of, row = device // 8, device // 2 % 4, device % 2, source % 12
    tab = jnp.stack([(z_of * 2 + c_of) * 12 + row, (y_of * 2 + c_of) * 12 + row])
    tab = jnp.broadcast_to(jnp.pad(tab, ((0, 0), (0, 116)))[:, None], (2, 8, 128))
    loc = jnp.stack([y_of, z_of, (rotation // 4).reshape(12)])
    vmem = pl.BlockSpec(memory_space=pltpu.VMEM)
    dma = pltpu.SemaphoreType.DMA
    out, gfeat, full1, full2 = pl.pallas_call(
        kernel,
        out_shape=(
            jax.ShapeDtypeStruct((3, 1024, 256), BF16),
            jax.ShapeDtypeStruct((3, 1024, 256), BF16),
            jax.ShapeDtypeStruct((2, 4, 4, 9, 16, 128), BF16),
            jax.ShapeDtypeStruct((2, 4, 4, 9, 16, 128), BF16),
        ),
        in_specs=[vmem] * 5 + [pl.BlockSpec(memory_space=pltpu.SMEM)],
        out_specs=(vmem,) * 4,
        scratch_shapes=[
            pltpu.VMEM((3, 1088, 768), BF16),
            pltpu.VMEM((3, 1088, 768), BF16),
            pltpu.VMEM((3, 1088, 768), BF16),
            pltpu.VMEM((3, 768, 256), BF16),
            pltpu.VMEM((3, 1024, 256), F32),
            pltpu.VMEM((3, 1024, 256), F32),
            pltpu.VMEM((3, 256, 1024), BF16),
            pltpu.VMEM((2, 4, 4, 9, 16, 128), F32),
            pltpu.VMEM((4, 96, 768), BF16),
            pltpu.VMEM((3, 4, 96, 256), BF16),
            pltpu.VMEM((2, 96, 32), BF16),
            pltpu.VMEM((4, 2, 12, 32, 128), BF16),
            *[pltpu.VMEM((96, 32, 128), BF16)] * 4,
            pltpu.VMEM((4, 8, 12, 32, 128), BF16),
            *[pltpu.VMEM((2, 4, 12, 32, 128), BF16)] * 4,
            pltpu.VMEM((8, 8, 128), jnp.int32),
            pltpu.SMEM((8, 8, 128), jnp.int32),
            pltpu.VMEM((96, 256), F32),
            pltpu.VMEM((2, 2, 4, 4, 9, 16, 128), BF16),
            pltpu.VMEM((2, 4, 4, 9, 16, 128), BF16),
            pltpu.VMEM((2, 4, 4, 9, 16, 128), BF16),
            pltpu.VMEM((2, 4, 4, 9, 16, 128), BF16),
            pltpu.VMEM((2, 4, 9, 16, 128), BF16),
            pltpu.VMEM((2, 4, 9, 16, 128), BF16),
            pltpu.VMEM((2, 9, 16, 128), BF16),
            pltpu.VMEM((2, 4, 9, 16, 128), BF16),
            dma((7,)),
            dma((8,)),
            dma((4, 7)),
            dma((4, 8)),
            dma((4, 7)),
            dma((4, 8)),
            dma((2, 22)),
            dma((2, 22)),
            dma((4,)),
        ],
        compiler_params=pltpu.CompilerParams(
            collective_id=0, has_side_effects=True, vmem_limit_bytes=67043328
        ),
    )(features[0], cotangent[0], conv_one, conv_two, tab, loc)

    def whole(full):
        return jnp.transpose(full.astype(F32) * factor, (3, 1, 2, 4, 0, 5)).reshape(3, 3, 256, 256)

    shape = features.shape
    return (out.reshape(shape), gfeat.reshape(shape), whole(full1), whole(full2))


def solution(mesh):
    placed = (
        P("members", "tiles", None, None, None),
        P(),
        P(),
        P("members", "tiles", None, None, None),
        P("tiles", None),
        P("tiles", None),
    )
    return jax.shard_map(
        on_device,
        mesh=mesh,
        in_specs=placed,
        out_specs=(
            P("members", "tiles", None, None, None),
            P("members", "tiles", None, None, None),
            P(),
            P(),
        ),
        check_vma=False,
    )
```

time: 442 us -> 163 us (0.37); the launches traced: 434 us -> 163 us
  waiting for transfers between devices: 258 us -> 0 us
  Pallas kernels: 0 us -> 140 us
  local copies, waits for them, and re-layouts: 80 us -> 18.9 us
  matrix products: 56.1 us -> 0 us
  other arithmetic: 24.4 us -> 3.53 us
  between operations: 14.8 us -> 0.68 us
    pallas_call x0 -> x1, Pallas kernels: none -> 140 us  [on_device(): pl.pallas_call(kernel, out_shape=(jax.ShapeDtypeStruct((3, 1024, 256), BF...]
    psum x1 -> x0, waiting for transfers between devices: 140 us -> none  [on_device(): first, second = lax.psum((first, second), ('tiles', 'members'))]
    all_gather x4 -> x0, waiting for transfers between devices: 118 us -> none  [the longest x2 80.5 us: return_rims(): lax.all_gather(rim_vals.reshape(-1, cells, chans), 'tiles', axis=0, tiled...]
    conv_general_dilated x6 -> x0, matrix products: 56.1 us -> none  [the longest x2 25.9 us: kernel_grad(): lax.conv_general_dilated(padded, gradient, (1, 1), 'VALID', dimension_num...]
    unnamed x75 -> x6, local copies, waits for them, and re-layouts: 25.9 us -> 3.12 us
    gather x8 -> x0, local copies, waits for them, and re-layouts: 17.4 us -> none  [seam_rows(): return orient(edge_list[source], rotation)]
    conv_general_dilated x11 -> x0, local copies, waits for them, and re-layouts: 11.7 us -> none  [the longest x7 10.1 us: spread(): lax.conv_general_dilated(gradient, turned, (1, 1), ((2, 2), (2, 2)), dime...]
    convert_element_type x3 -> x0, other arithmetic: 10.8 us -> none  [the longest x1 8.45 us: on_device(): (d_act * sigmoid_v * (1.0 + preact * (1.0 - sigmoid_v))).astype(jnp.bfloa...]
  transfers between devices with their start and end apart: 5 -> 0, of which waited for: 4 -> 0; matrix products, arithmetic and copies ran while one was open for 21% -> 0% of each run, Pallas kernels for 0% -> 0%
where the time goes in v1:
time: 163 us
  Pallas kernels  140 us (86%)
  local copies, waits for them, and re-layouts  18.9 us (12%)
  other arithmetic  3.53 us (2%)
    pallas_call x1, Pallas kernels, on_device(): pl.pallas_call(kernel, out_shape=(jax.ShapeDtypeStruct((3, 1024, 256), BF...  140 us
    reshape x2, local copies, waits for them, and re-layouts, whole(): jnp.transpose(full.astype(F32) * factor, (3, 1, 2, 4, 0, 5))  8.41 us
    transpose x2, local copies, waits for them, and re-layouts, whole(): jnp.transpose(full.astype(F32) * factor, (3, 1, 2, 4, 0, 5))  6.45 us

profile of v1, /device:TPU:1, one launch (start us, length us, event | category | flops | bytes accessed | tf_op | source)
XLA Modules:
  0.0 163.1 jit_solution(12009777786736136359)
XLA Ops:
  0.6 0.7 broadcast_remainder_fusion
  1.3 0.1 rem.115
  1.4 0.1 stack_reshape.3
  1.5 0.1 div.59
  1.6 0.1 ne.194
  1.8 0.6 pad_add_fusion.loc
  2.4 0.6 broadcast_in_dim.2.tab
  3.0 140.0 %shard_map.93 = (bf16[3,1024,256]{2,1,0:T(8,128)(2,1)}, bf16[3,1024,256]{2,1,0:T(8,128)(2,1)}, bf16[2,4,4,9,16,128]{5,4,3,2,1,0:T(8,128)(2,1)}, bf16[2,4,4,9,16,128]{5,4,3,2,1,0:T(8,128)(2,1)}) custom-call(bf16[3,32,32,256]{3,2,1,0:T(8,128)(2,1)} %bitcast.10, bf16[3,32,32,256]{3,2,1,0:T(8,128)(2,1)} %bitcast.11, bf16[3,3,256,256]{3,2,1,0:T(8,128)(2,1)} %w1.1, ...), custom_call_target="tpu_custom_call" | custom-call | tf_op jit(solution)/shard_map/pallas_call | solution.py:458
  143.0 2.2 %multiply_bitcast_fusion = (f32[9,4,4,16,2,128]{5,3,0,2,1,4:T(8,128)S(1)}, f32[9,4,4,16,2,128]{5,3,0,2,1,4:T(8,128)S(1)}) fusion(bf16[2,4,4,9,16,128]{5,4,3,2,1,0:T(8,128)(2,1)} %get-tuple-element.11, bf16[2,4,4,9,16,128]{5,4,3,2,1,0:T(8,128)(2,1)} %get-tuple-element.10), kind=kLoop, calls=%fused_computation | loop fusion | flops 2359296 | bytes 7077888 | tf_op jit(solution)/shard_map/transpose | solution.py:511
  145.1 3.2 %copy.11 = f32[9,4,4,16,2,128]{5,4,3,2,1,0:T(2,128)} copy(f32[9,4,4,16,2,128]{5,3,0,2,1,4:T(8,128)S(1)} %get-tuple-element.21) | data formatting | bytes 4718592 | tf_op jit(solution)/shard_map/transpose | solution.py:511
  148.3 4.1 %reshape.268 = f32[3,3,256,256]{3,2,1,0:T(8,128)} reshape(f32[9,4,4,16,2,128]{5,4,3,2,1,0:T(2,128)} %copy.11) | data formatting | bytes 4718592 | tf_op jit(solution)/shard_map/reshape | solution.py:511
  152.5 3.2 %copy.10 = f32[9,4,4,16,2,128]{5,4,3,2,1,0:T(2,128)} copy(f32[9,4,4,16,2,128]{5,3,0,2,1,4:T(8,128)S(1)} %get-tuple-element.22) | data formatting | bytes 4718592 | tf_op jit(solution)/shard_map/transpose | solution.py:511
  155.7 0.0 copy-start.1
  155.7 4.3 %reshape.267 = f32[3,3,256,256]{3,2,1,0:T(8,128)} reshape(f32[9,4,4,16,2,128]{5,4,3,2,1,0:T(2,128)} %copy.10) | data formatting | bytes 4718592 | tf_op jit(solution)/shard_map/reshape | solution.py:511
  160.0 0.0 copy-done.1
  160.0 0.0 copy-start
  160.0 1.1 copy.14
  161.1 0.8 copy-done
  162.0 1.1 copy.15
  (6 shorter events, 0.1 us)
Async XLA Ops:
  155.7 4.3 %copy-start.1 = (bf16[3,1024,256]{2,1,0:T(8,128)(2,1)S(1)}, bf16[3,1024,256]{2,1,0:T(8,128)(2,1)}, u32[]{:S(2)}) copy-start(bf16[3,1024,256]{2,1,0:T(8,128)(2,1)} %get-tuple-element.8) | copy-start | bytes 4718596
  160.0 2.0 %copy-start = (bf16[3,1024,256]{2,1,0:T(8,128)(2,1)S(1)}, bf16[3,1024,256]{2,1,0:T(8,128)(2,1)}, u32[]{:S(2)}) copy-start(bf16[3,1024,256]{2,1,0:T(8,128)(2,1)} %get-tuple-element.9) | copy-start | bytes 4718596

commit v2 on v1

v2 whole, which is shorter than its diff:
```python
import functools
import math

import jax
import jax.numpy as jnp
from jax import lax
from jax.experimental import pallas as pl
from jax.experimental.pallas import tpu as pltpu
from jax.sharding import PartitionSpec as P

MESH = pl.DeviceIdType.MESH
F32 = jnp.float32
BF16 = jnp.bfloat16
ROWS = 512


ORDER = ("xyz", "yzx", "zxy")


def kernel(
    feat_hbm, cot_hbm, w1_hbm, w2_hbm, tab, loc,
    out, gfeat, gout1, gout2,
    feat, cot, w1, w2,
    fa3, c3, d3, wt, pre, dact, xt, grad1, grad2, seams, edges, rimrows, corr, mats, pickrow,
    edge_out, ag0, ag1, ag2, ag3, pick, got0, got1, got2, got3, tabv, tabs,
    snd, rcore, sx, rx, sy, ry, sz, rz, full,
    tab_s, tab_r, ag_s, ag_r, pk_s, pk_r, ar_s, ar_r, loc_sem, in_sem,
):
    ag = (ag0, ag1, ag2, ag3)
    got = (got0, got1, got2, got3)
    grads = (grad1, grad2)
    gouts = (gout1, gout2)
    loads = [
        pltpu.make_async_copy(src, dst, in_sem.at[i])
        for i, (src, dst) in enumerate(((feat_hbm, feat), (cot_hbm, cot), (w2_hbm, w2), (w1_hbm, w1)))
    ]
    for copy in loads:
        copy.start()
    me = lax.axis_index("tiles")
    xpos = lax.axis_index("members")
    core = lax.rem(me, 2)
    ypos = lax.rem(me // 2, 4)
    zpos = me // 8
    pos = {"x": xpos, "y": ypos, "z": zpos}
    ring = zpos * (1 - core) + ypos * core
    other = ypos * (1 - core) + zpos * core

    def tid(z, y, c):
        return (z * 4 + y) * 2 + c

    partner = tid(zpos, ypos, 1 - core)

    def wrap(v):
        return lax.rem(v, 4)

    barrier = pltpu.get_barrier_semaphore()
    pl.semaphore_signal(barrier, inc=1, device_id={"tiles": partner}, device_id_type=MESH)
    for d in range(1, 4):
        for c in range(2):
            pl.semaphore_signal(barrier, inc=1, device_id={"tiles": tid(wrap(zpos + d), ypos, c)}, device_id_type=MESH)
            pl.semaphore_signal(barrier, inc=1, device_id={"tiles": tid(zpos, wrap(ypos + d), c)}, device_id_type=MESH)
        pl.semaphore_signal(barrier, inc=1, device_id={"members": wrap(xpos + d)}, device_id_type=MESH)

    r_i = lax.broadcasted_iota(jnp.int32, (128, 1024), 0)
    c_i = lax.broadcasted_iota(jnp.int32, (128, 1024), 1)
    e_i = r_i // 32
    k_i = r_i - e_i * 32
    want = jnp.where(e_i == 0, k_i, jnp.where(e_i == 1, 992 + k_i, jnp.where(e_i == 2, 32 * k_i, 32 * k_i + 31)))
    pickrow[...] = jnp.where(c_i == want, 1.0, 0.0).astype(BF16)
    m_r = lax.broadcasted_iota(jnp.int32, (288, 96), 0)
    m_c = lax.broadcasted_iota(jnp.int32, (288, 96), 1)
    m_b = m_r // 96
    m_t = (m_r - m_b * 96) // 32
    m_j = m_r - m_b * 96 - m_t * 32 + m_b - 1
    inside = (m_j >= 0) & (m_j < 32)
    mats[0] = jnp.where(inside & (m_c == m_t * 32 + m_j), 1.0, 0.0)
    mats[1] = jnp.where(inside & (m_c == m_t * 32 + 31 - m_j), 1.0, 0.0)
    tile_of = m_t

    pl.semaphore_wait(barrier, 16)

    def remote(src, dst, ssem, rsem, target):
        return pltpu.make_async_remote_copy(
            src_ref=src, dst_ref=dst, send_sem=ssem, recv_sem=rsem,
            device_id={"tiles": target}, device_id_type=MESH,
        )

    def remote_x(src, dst, ssem, rsem, target):
        return pltpu.make_async_remote_copy(
            src_ref=src, dst_ref=dst, send_sem=ssem, recv_sem=rsem,
            device_id={"members": target}, device_id_type=MESH,
        )

    sends = []

    def launch(make):
        make().start()
        sends.append(make)

    for d in range(1, 4):
        launch(lambda d=d: remote(tab.at[0], tabv.at[ypos * 2 + core], tab_s.at[d - 1], tab_r.at[ypos * 2 + core], tid(zpos, wrap(ypos + d), 0)))
        launch(lambda d=d: remote(tab.at[1], tabv.at[zpos * 2 + core], tab_s.at[d + 2], tab_r.at[zpos * 2 + core], tid(wrap(zpos + d), ypos, 1)))
    slot_p = (ypos * core + zpos * (1 - core)) * 2 + core
    launch(lambda: remote(tab.at[1 - core], tabv.at[slot_p], tab_s.at[6], tab_r.at[slot_p], partner))
    tab_own = pltpu.make_async_copy(tab.at[core], tabv.at[other * 2 + core], loc_sem.at[0])
    tab_own.start()

    def dot(a, b):
        return jnp.dot(a, b, preferred_element_type=F32)

    def dot_nt(a, b):
        return lax.dot_general(a, b, (((1,), (1,)), ((), ())), preferred_element_type=F32)

    def dot_tn(a, b):
        return lax.dot_general(a, b, (((0,), (0,)), ((), ())), preferred_element_type=F32)

    def take_edges(get, which):
        for t in range(3):
            picked = dot(pickrow[...], get(t)).astype(BF16)
            for e in range(4):
                edges[which, e, t * 32:t * 32 + 32, :] = picked[e * 32:e * 32 + 32]

    def put_edge(n, t, e, value):
        edge_out[n, 0, t * 4 + e] = value[:, 0:128]
        edge_out[n, 1, t * 4 + e] = value[:, 128:256]

    def put_edges(n, which):
        for t in range(3):
            for e in range(4):
                put_edge(n, t, e, edges[which, e, t * 32:t * 32 + 32, :])

    def send_edges(n):
        for d in range(1, 4):
            launch(lambda d=d: remote(edge_out.at[n, 0], ag[n].at[pl.ds((zpos * 2 + core) * 12, 12)], ag_s.at[n, d - 1], ag_r.at[n, zpos * 2 + core], tid(wrap(zpos + d), ypos, 0)))
            launch(lambda d=d: remote(edge_out.at[n, 1], ag[n].at[pl.ds((ypos * 2 + core) * 12, 12)], ag_s.at[n, d + 2], ag_r.at[n, ypos * 2 + core], tid(zpos, wrap(ypos + d), 1)))
        slot = (zpos * core + ypos * (1 - core)) * 2 + core
        launch(lambda: remote(edge_out.at[n, 1 - core], ag[n].at[pl.ds(slot * 12, 12)], ag_s.at[n, 6], ag_r.at[n, slot], partner))
        own = pltpu.make_async_copy(edge_out.at[n, core], ag[n].at[pl.ds((ring * 2 + core) * 12, 12)], loc_sem.at[1])
        own.start()
        own.wait()

    def forward(n):
        def wait(slot):
            remote(edge_out.at[n, 0], ag[n].at[pl.ds(slot * 12, 12)], ag_s.at[n, 0], ag_r.at[n, slot], partner).wait_recv()

        for d in range(1, 4):
            for c in range(2):
                wait(wrap(ring + d) * 2 + c)
        wait(ring * 2 + 1 - core)

        def choose(q, carry):
            for k in range(12):
                pick[n, q, k] = ag[n][tabs[q, 0, k]]
            return carry

        lax.fori_loop(0, 8, choose, 0)

        def one(d, c):
            p = wrap(other + d)
            target = tid(zpos * (1 - core) + p * core, p * (1 - core) + ypos * core, c)
            return remote(pick.at[n, p * 2 + c], got[n].at[core, other], pk_s.at[n, d * 2 + c - 2], pk_r.at[n, core * 4 + other], target)

        for d in range(1, 4):
            for c in range(2):
                launch(lambda d=d, c=c: one(d, c))
        launch(lambda: remote(pick.at[n, other * 2 + 1 - core], got[n].at[core, other], pk_s.at[n, 6], pk_r.at[n, core * 4 + other], partner))
        own = pltpu.make_async_copy(pick.at[n, other * 2 + core], got[n].at[core, other], loc_sem.at[2])
        own.start()
        own.wait()

    def arrive(n):
        def wait(h, p):
            remote(pick.at[n, 0], got[n].at[h, p], pk_s.at[n, 0], pk_r.at[n, h * 4 + p], partner).wait_recv()

        for d in range(1, 4):
            wait(0, wrap(ypos + d))
            wait(1, wrap(zpos + d))
        wait(1 - core, zpos * (1 - core) + ypos * core)

    def received(n, e):
        rows = []
        for t in range(3):
            k = t * 4 + e
            rows.append(jnp.concatenate([got[n][0, loc[0, k], k], got[n][1, loc[1, k], k]], axis=1))
        return jnp.concatenate(rows, axis=0)

    def turned(e, low, high):
        flip = jnp.where(tile_of == 0, loc[2, e], jnp.where(tile_of == 1, loc[2, 4 + e], loc[2, 8 + e]))[low:high]
        return jnp.where(flip == 1, mats[1, low:high], mats[0, low:high]).astype(BF16)

    def take_seams(n):
        for e in range(4):
            both = dot(turned(e, 0, 288), received(n, e)).astype(BF16)
            for b in range(3):
                seams[e, :, b * 256:b * 256 + 256] = both[b * 96:b * 96 + 96]

    jj = lax.rem(lax.broadcasted_iota(jnp.int32, (128, 256), 0), 32)

    def put3(dst, t, r, x):
        row = pl.multiple_of(32 + r * 128, 32)
        dst[t, pl.ds(row, 128), 256:512] = x.astype(BF16)
        dst[t, pl.ds(row, 128), 0:256] = jnp.where(jj == 0, 0.0, pltpu.roll(x, 1, 0)).astype(BF16)
        dst[t, pl.ds(row, 128), 512:768] = jnp.where(jj == 31, 0.0, pltpu.roll(x, 127, 0)).astype(BF16)

    def each_chunk(body):
        def step(i, carry):
            t = i // 8
            body(t, i - t * 8)
            return carry

        lax.fori_loop(0, 24, step, 0)

    def conv3(x3, weight, store, after=()):
        parts = 1024 // ROWS

        def step(i, carry):
            t = i // parts
            r = (i - t * parts) * ROWS
            acc = dot(x3[t, pl.ds(pl.multiple_of(r, 32), ROWS), :], weight(0))
            acc = acc + dot(x3[t, pl.ds(pl.multiple_of(r + 32, 32), ROWS), :], weight(1))
            acc = acc + dot(x3[t, pl.ds(pl.multiple_of(r + 64, 32), ROWS), :], weight(2))
            store(t, pl.multiple_of(r, 128), acc)
            for at, do in after:
                pl.when(i == at)(do)
            return carry

        lax.fori_loop(0, 3 * parts, step, 0)

    def edge_weight(w, e):
        return [w[0, 0], w[0, 1], w[0, 2]] if e == 0 else [w[2, 0], w[2, 1], w[2, 2]] if e == 1 else [w[0, 0], w[1, 0], w[2, 0]] if e == 2 else [w[0, 2], w[1, 2], w[2, 2]]

    eight = lax.broadcasted_iota(jnp.int32, (8, 256), 0)

    def add_edges(dst, value_of):
        for t in range(3):
            dst[t, 0:32, :] += value_of[0, t * 32:t * 32 + 32, :]
            dst[t, 992:1024, :] += value_of[1, t * 32:t * 32 + 32, :]

        def step(i, carry):
            for t in range(3):
                row = pl.multiple_of(i * 32, 8)
                line = jnp.broadcast_to(value_of[2, pl.ds(t * 32 + i, 1), :], (8, 256))
                dst[t, pl.ds(row, 8), :] += jnp.where(eight == 0, line, 0.0)
                row = pl.multiple_of(i * 32 + 24, 8)
                line = jnp.broadcast_to(value_of[3, pl.ds(t * 32 + i, 1), :], (8, 256))
                dst[t, pl.ds(row, 8), :] += jnp.where(eight == 7, line, 0.0)
            return carry

        lax.fori_loop(0, 32, step, 0)

    def seam_conv(w, dst):
        for e in range(4):
            ws = edge_weight(w, e)
            corr[e] = dot(seams[e, :, 0:256], ws[0]) + dot(seams[e, :, 256:512], ws[1]) + dot(seams[e, :, 512:768], ws[2])
        add_edges(dst, corr)

    def rim_add(n, dst):
        for e in range(4):
            corr[e] = dot(turned(e, 96, 192), received(n, e))
        add_edges(dst, corr)

    def rims(which, w, n):
        shift = mats[0].astype(BF16)
        for e in range(4):
            ws = edge_weight(w, e)
            rimrows[...] = dot(shift, edges[which, e]).astype(BF16)
            value = dot_nt(rimrows[192:288], ws[0]) + dot_nt(rimrows[96:192], ws[1]) + dot_nt(rimrows[0:96], ws[2])
            value = value.astype(BF16)
            for t in range(3):
                put_edge(n, t, e, value[t * 32:t * 32 + 32])

    def transpose_tiles(x3):
        eye = jnp.where(lax.broadcasted_iota(jnp.int32, (256, 256), 0) == lax.broadcasted_iota(jnp.int32, (256, 256), 1), 1.0, 0.0).astype(BF16)
        for t in range(3):
            xt[t] = dot_nt(eye, x3[t, 32:1056, 256:512]).astype(BF16)

    def turn_weight(w):
        for a in range(3):
            for b in range(3):
                wt[a, b * 256:b * 256 + 256, :] = w[2 - a, 2 - b].T

    def grad_inner(g3, dst):
        def step(i, carry):
            al = i // 3
            be = i - al * 3
            value = None
            for t in range(3):
                part = dot(xt[t], g3[t, pl.ds(pl.multiple_of(al * 32, 32), 1024), pl.ds(pl.multiple_of(be * 256, 256), 256)])
                value = part if value is None else value + part
            for h in range(2):
                dst[h, :, :, 8 - i] = value[:, h * 128:h * 128 + 128].reshape(4, 4, 16, 128)
            return carry

        lax.fori_loop(0, 9, step, 0)

    def grad_seams(which, dst):
        for e in range(4):
            value = dot_tn(seams[e], edges[which, e])
            for b in range(3):
                ab = (b, 6 + b, 3 * b, 3 * b + 2)[e]
                for h in range(2):
                    dst[h, :, :, ab] += value[b * 256:b * 256 + 256, h * 128:h * 128 + 128].reshape(4, 4, 16, 128)

    def along(axis, p, src, dst, ssem, rsem):
        if axis == "x":
            return remote_x(src, dst, ssem, rsem, p)
        return remote(src, dst, ssem, rsem, tid(zpos, p, core) if axis == "y" else tid(p, ypos, core))

    def swap(u, axis, base, src_of, dst_of):
        mine = pos[axis]
        for d in range(1, 4):
            def make(d=d):
                p = wrap(pos[axis] + d)
                return along(axis, p, src_of(p), dst_of(pos[axis]), ar_s.at[u, base + d - 1], ar_r.at[u, base + pos[axis]])

            launch(make)

    def swapped(u, axis, base, src_of, dst_of):
        for d in range(1, 4):
            p = wrap(pos[axis] + d)
            along(axis, p, src_of(p), dst_of(p), ar_s.at[u, base], ar_r.at[u, base + p]).wait_recv()

    def core_args(u):
        return (snd.at[u], rcore.at[u], ar_s.at[u, 0], ar_r.at[u, 0], partner)

    def first_args(u, r):
        return (u, ORDER[r][0], 1, lambda p: sx.at[u, p], lambda p: rx.at[u, p])

    def second_args(u, r):
        return (u, ORDER[r][1], 5, lambda p: sy.at[u, p], lambda p: ry.at[u, p])

    def third_args(u, r):
        return (u, ORDER[r][2], 9, lambda p: sz.at[u], lambda p: rz.at[u, p])

    def back_second_args(u, r):
        return (u, ORDER[r][1], 13, lambda p: full.at[u, core, pos[ORDER[r][0]], pos[ORDER[r][1]]], lambda p: full.at[u, core, pos[ORDER[r][0]], p])

    def back_first_args(u, r):
        return (u, ORDER[r][0], 17, lambda p: full.at[u, core, pos[ORDER[r][0]]], lambda p: full.at[u, core, p])

    def step_core(g):
        for r in range(3):
            u = g * 3 + r
            snd[u] = grads[g][1 - core, :, :, 3 * r:3 * r + 3].astype(BF16)
            launch(lambda u=u: remote(*core_args(u)))

    def step_first(g):
        for r in range(3):
            u = g * 3 + r
            remote(*core_args(u)).wait_recv()
            sx[u] = (grads[g][core, :, :, 3 * r:3 * r + 3] + rcore[u].astype(F32)).astype(BF16)
            swap(*first_args(u, r))

    def step_second(g):
        for r in range(3):
            u = g * 3 + r
            swapped(*first_args(u, r))
            mine = pos[ORDER[r][0]]
            total = grads[g][core, mine, :, 3 * r:3 * r + 3] + rcore[u, mine].astype(F32)
            for d in range(1, 4):
                total = total + rx[u, wrap(mine + d)].astype(F32)
            sy[u] = total.astype(BF16)
            swap(*second_args(u, r))

    def step_third(g):
        for r in range(3):
            u = g * 3 + r
            swapped(*second_args(u, r))
            mine = pos[ORDER[r][1]]
            total = sy[u, mine].astype(F32)
            for d in range(1, 4):
                total = total + ry[u, wrap(mine + d)].astype(F32)
            sz[u] = total
            swap(*third_args(u, r))

    def step_back_second(g):
        for r in range(3):
            u = g * 3 + r
            swapped(*third_args(u, r))
            total = sz[u]
            mine = pos[ORDER[r][2]]
            rz[u, mine] = total
            total = (rz[u, 0] + rz[u, 1]) + (rz[u, 2] + rz[u, 3])
            full[u, core, pos[ORDER[r][0]], pos[ORDER[r][1]]] = total.astype(BF16)
            swap(*back_second_args(u, r))

    def step_back_first(g):
        for r in range(3):
            u = g * 3 + r
            swapped(*back_second_args(u, r))
            swap(*back_first_args(u, r))

    def last_args(u, h):
        return (full.at[u, h], full.at[u, h], ar_s.at[u, 21], ar_r.at[u, 21], partner)

    def step_back_core(g):
        for r in range(3):
            u = g * 3 + r
            swapped(*back_first_args(u, r))
            launch(lambda u=u: remote(*last_args(u, core)))

    def step_end(g):
        for r in range(3):
            u = g * 3 + r
            remote(*last_args(u, 1 - core)).wait_recv()
            for b in range(3):
                for h in range(2):
                    gouts[g][3 * r + b, :, h * 128:h * 128 + 128] = full[u, h, :, :, b].reshape(256, 128)

    loads[0].wait()
    take_edges(lambda t: feat[t].reshape(1024, 256), 0)
    put_edges(0, 0)
    send_edges(0)
    loads[1].wait()
    loads[2].wait()
    take_edges(lambda t: cot[t].reshape(1024, 256), 1)
    rims(1, w2, 1)
    send_edges(1)

    for x3 in (fa3, c3, d3):
        x3[:, 0:32, :] = jnp.zeros((3, 32, 768), BF16)
        x3[:, 1056:1088, :] = jnp.zeros((3, 32, 768), BF16)

    def load_feat(t, r):
        put3(fa3, t, r, feat[t, pl.ds(r * 4, 4)].reshape(128, 256).astype(F32))

    def load_cot(t, r):
        put3(c3, t, r, cot[t, pl.ds(r * 4, 4)].reshape(128, 256).astype(F32))

    each_chunk(load_feat)
    for d in range(1, 4):
        for c in range(2):
            slot = wrap(other + d) * 2 + c
            remote(tab.at[0], tabv.at[slot], tab_s.at[0], tab_r.at[slot], partner).wait_recv()
    slot = other * 2 + 1 - core
    remote(tab.at[0], tabv.at[slot], tab_s.at[0], tab_r.at[slot], partner).wait_recv()
    tab_own.wait()
    to_smem = pltpu.make_async_copy(tabv, tabs, loc_sem.at[3])
    to_smem.start()
    to_smem.wait()

    def store_pre(t, r, acc):
        pre[t, pl.ds(r, ROWS), :] = acc

    def store_dact(t, r, acc):
        dact[t, pl.ds(r, ROWS), :] = acc

    loads[3].wait()
    conv3(fa3, lambda a: w1[a].reshape(768, 256), store_pre)
    forward(0)
    each_chunk(load_cot)
    turn_weight(w2)
    forward(1)
    conv3(c3, lambda a: wt[a], store_dact)
    transpose_tiles(fa3)
    turn_weight(w1)
    arrive(0)
    take_seams(0)
    seam_conv(w1, pre)

    def activate(t, r):
        row = pl.multiple_of(r * 128, 128)
        u = pre[t, pl.ds(row, 128), :]
        s = 1.0 / (1.0 + jnp.exp(-u))
        put3(fa3, t, r, (u * s).astype(BF16).astype(F32))
        pre[t, pl.ds(row, 128), :] = s * (1.0 + u * (1.0 - s))

    each_chunk(activate)

    take_edges(lambda t: fa3[t, 32:1056, 256:512], 2)
    put_edges(2, 2)
    send_edges(2)
    arrive(1)
    rim_add(1, dact)

    def slope(t, r):
        row = pl.multiple_of(r * 128, 128)
        d = dact[t, pl.ds(row, 128), :] * pre[t, pl.ds(row, 128), :]
        put3(d3, t, r, d.astype(BF16).astype(F32))

    each_chunk(slope)
    take_edges(lambda t: d3[t, 32:1056, 256:512], 0)
    rims(0, w1, 3)
    send_edges(3)
    grad_inner(d3, grad1)
    grad_seams(0, grad1)
    step_core(0)
    forward(2)
    transpose_tiles(fa3)
    step_first(0)
    grad_inner(c3, grad2)
    step_second(0)
    forward(3)
    arrive(2)
    take_seams(2)
    grad_seams(1, grad2)
    step_core(1)
    step_third(0)

    def after_a():
        step_first(1)
        step_back_second(0)

    def after_b():
        step_second(1)
        step_back_first(0)

    def after_c():
        step_third(1)
        step_back_core(0)

    conv3(fa3, lambda a: w2[a].reshape(768, 256), store_pre, ((1, after_a), (4, after_b)))
    seam_conv(w2, pre)
    after_c()

    def finish_out(t, r):
        row = pl.multiple_of(r * 128, 128)
        out[t, pl.ds(row, 128), :] = pre[t, pl.ds(row, 128), :].astype(BF16)

    def finish_gfeat(t, r):
        row = pl.multiple_of(r * 128, 128)
        gfeat[t, pl.ds(row, 128), :] = dact[t, pl.ds(row, 128), :].astype(BF16)

    each_chunk(finish_out)
    conv3(d3, lambda a: wt[a], store_dact, ((0, lambda: step_back_second(1)), (2, lambda: step_back_first(1)), (5, lambda: step_back_core(1))))
    step_end(0)
    arrive(3)
    rim_add(3, dact)
    each_chunk(finish_gfeat)
    step_end(1)
    for make in sends:
        make().wait_send()


def on_device(features, conv_one, conv_two, cotangent, neighbour_tile, rotation):
    cells_all = lax.axis_size("members") * lax.axis_size("tiles") * 3 * 1024
    factor = 1.0 / math.sqrt(cells_all)
    source = (4 * neighbour_tile + rotation % 4).reshape(12)
    device = source // 12
    z_of, y_of, c_of, row = device // 8, device // 2 % 4, device % 2, source % 12
    tab = jnp.stack([(z_of * 2 + c_of) * 12 + row, (y_of * 2 + c_of) * 12 + row])
    tab = jnp.broadcast_to(jnp.pad(tab, ((0, 0), (0, 116)))[:, None], (2, 8, 128))
    loc = jnp.stack([y_of, z_of, (rotation // 4).reshape(12)])
    vmem = pl.BlockSpec(memory_space=pltpu.VMEM)
    dma = pltpu.SemaphoreType.DMA
    out, gfeat, gout1, gout2 = pl.pallas_call(
        kernel,
        out_shape=(
            jax.ShapeDtypeStruct((3, 1024, 256), BF16),
            jax.ShapeDtypeStruct((3, 1024, 256), BF16),
            jax.ShapeDtypeStruct((9, 256, 256), BF16),
            jax.ShapeDtypeStruct((9, 256, 256), BF16),
        ),
        in_specs=[pl.BlockSpec(memory_space=pl.ANY)] * 4 + [vmem] + [pl.BlockSpec(memory_space=pltpu.SMEM)],
        out_specs=(vmem,) * 4,
        scratch_shapes=[
            pltpu.VMEM((3, 32, 32, 256), BF16),
            pltpu.VMEM((3, 32, 32, 256), BF16),
            pltpu.VMEM((3, 3, 256, 256), BF16),
            pltpu.VMEM((3, 3, 256, 256), BF16),
            pltpu.VMEM((3, 1088, 768), BF16),
            pltpu.VMEM((3, 1088, 768), BF16),
            pltpu.VMEM((3, 1088, 768), BF16),
            pltpu.VMEM((3, 768, 256), BF16),
            pltpu.VMEM((3, 1024, 256), F32),
            pltpu.VMEM((3, 1024, 256), F32),
            pltpu.VMEM((3, 256, 1024), BF16),
            pltpu.VMEM((2, 4, 4, 9, 16, 128), F32),
            pltpu.VMEM((2, 4, 4, 9, 16, 128), F32),
            pltpu.VMEM((4, 96, 768), BF16),
            pltpu.VMEM((3, 4, 96, 256), BF16),
            pltpu.VMEM((288, 256), BF16),
            pltpu.VMEM((4, 96, 256), F32),
            pltpu.VMEM((2, 288, 96), F32),
            pltpu.VMEM((128, 1024), BF16),
            pltpu.VMEM((4, 2, 12, 32, 128), BF16),
            *[pltpu.VMEM((96, 32, 128), BF16)] * 4,
            pltpu.VMEM((4, 8, 12, 32, 128), BF16),
            *[pltpu.VMEM((2, 4, 12, 32, 128), BF16)] * 4,
            pltpu.VMEM((8, 8, 128), jnp.int32),
            pltpu.SMEM((8, 8, 128), jnp.int32),
            pltpu.VMEM((6, 4, 4, 3, 16, 128), BF16),
            pltpu.VMEM((6, 4, 4, 3, 16, 128), BF16),
            pltpu.VMEM((6, 4, 4, 3, 16, 128), BF16),
            pltpu.VMEM((6, 4, 4, 3, 16, 128), BF16),
            pltpu.VMEM((6, 4, 3, 16, 128), BF16),
            pltpu.VMEM((6, 4, 3, 16, 128), BF16),
            pltpu.VMEM((6, 3, 16, 128), F32),
            pltpu.VMEM((6, 4, 3, 16, 128), F32),
            pltpu.VMEM((6, 2, 4, 4, 3, 16, 128), BF16),
            dma((7,)),
            dma((8,)),
            dma((4, 7)),
            dma((4, 8)),
            dma((4, 7)),
            dma((4, 8)),
            dma((6, 22)),
            dma((6, 22)),
            dma((4,)),
            dma((4,)),
        ],
        compiler_params=pltpu.CompilerParams(
            collective_id=0, has_side_effects=True, vmem_limit_bytes=67043328
        ),
    )(features[0], cotangent[0], conv_one, conv_two, tab, loc)

    def whole(total):
        return (total.astype(F32) * factor).reshape(3, 3, 256, 256)

    shape = features.shape
    return (out.reshape(shape), gfeat.reshape(shape), whole(gout1), whole(gout2))


def solution(mesh):
    placed = (
        P("members", "tiles", None, None, None),
        P(),
        P(),
        P("members", "tiles", None, None, None),
        P("tiles", None),
        P("tiles", None),
    )
    return jax.shard_map(
        on_device,
        mesh=mesh,
        in_specs=placed,
        out_specs=(
            P("members", "tiles", None, None, None),
            P("members", "tiles", None, None, None),
            P(),
            P(),
        ),
        check_vma=False,
    )
```

time: 163 us -> 96.8 us (0.59)
  Pallas kernels: 140 us -> 86 us
  local copies, waits for them, and re-layouts: 18.9 us -> 4.06 us
  other arithmetic: 3.53 us -> 5.84 us
    pallas_call x1, Pallas kernels: 140 us -> 86 us  [on_device(): pl.pallas_call(kernel, out_shape=(jax.ShapeDtypeStruct((3, 1024, 256), BF...]
    reshape x2 -> x0, local copies, waits for them, and re-layouts: 8.41 us -> none  [whole(): jnp.transpose(full.astype(F32) * factor, (3, 1, 2, 4, 0, 5))]
    transpose x2 -> x0, local copies, waits for them, and re-layouts: 6.45 us -> none  [whole(): jnp.transpose(full.astype(F32) * factor, (3, 1, 2, 4, 0, 5))]
    mul x0 -> x1, other arithmetic: none -> 4.47 us  [whole(): return (total.astype(F32) * factor).reshape(3, 3, 256, 256)]
    transpose x1 -> x0, other arithmetic: 2.16 us -> none  [whole(): jnp.transpose(full.astype(F32) * factor, (3, 1, 2, 4, 0, 5))]
where the time goes in v2:
time: 96.8 us; the launch traced here: 96.6 us
  Pallas kernels  86 us (89%)
  other arithmetic  5.84 us (6%)
  local copies, waits for them, and re-layouts  4.06 us (4%)
    pallas_call x1, Pallas kernels, on_device(): pl.pallas_call(kernel, out_shape=(jax.ShapeDtypeStruct((3, 1024, 256), BF...  86 us
    mul x1, other arithmetic, whole(): return (total.astype(F32) * factor).reshape(3, 3, 256, 256)  4.47 us
    unnamed x6, local copies, waits for them, and re-layouts  3.12 us

profile of v2, /device:TPU:1, one launch (start us, length us, event | category | flops | bytes accessed | tf_op | source)
XLA Modules:
  0.0 96.6 jit_solution(5268751360669284494)
XLA Ops:
  0.6 0.7 broadcast_remainder_fusion
  1.3 0.1 rem.115
  1.4 0.1 stack_reshape.3
  1.5 0.1 div.59
  1.6 0.1 ne.194
  1.8 0.6 pad_add_fusion.loc
  2.4 0.6 broadcast_in_dim.2.tab
  3.0 86.0 %shard_map.93 = (bf16[3,1024,256]{2,1,0:T(8,128)(2,1)}, bf16[3,1024,256]{2,1,0:T(8,128)(2,1)}, bf16[9,256,256]{2,1,0:T(8,128)(2,1)}, bf16[9,256,256]{2,1,0:T(8,128)(2,1)}) custom-call(bf16[3,32,32,256]{3,2,1,0:T(8,128)(2,1)} %bitcast.10, bf16[3,32,32,256]{3,2,1,0:T(8,128)(2,1)} %bitcast.11, bf16[3,3,256,256]{3,2,1,0:T(8,128)(2,1)} %w1_hbm.1, ...), custom_call_target="tpu_custom_call" | custom-call | tf_op jit(solution)/shard_map/pallas_call | solution.py:546
  89.0 0.0 copy-start.1
  89.0 4.5 %convert_multiply_fusion = (f32[9,256,256]{2,1,0:T(8,128)}, f32[9,256,256]{2,1,0:T(8,128)}) fusion(bf16[9,256,256]{2,1,0:T(8,128)(2,1)} %get-tuple-element.11, bf16[9,256,256]{2,1,0:T(8,128)(2,1)} %get-tuple-element.10), kind=kLoop, calls=%fused_computation | loop fusion | flops 2359296 | bytes 7077888 | tf_op jit(solution)/shard_map/mul | solution.py:608
  93.4 0.0 copy-done.1
  93.4 0.0 copy-start
  93.4 1.1 %copy.12 = bf16[1,3,32,32,256]{4,3,2,1,0:T(8,128)(2,1)} copy(bf16[1,3,32,32,256]{4,3,2,1,0:T(8,128)(2,1)S(1)} %bitcast.9) | data formatting | bytes 3145728
  94.6 0.8 copy-done
  95.4 1.1 %copy.13 = bf16[1,3,32,32,256]{4,3,2,1,0:T(8,128)(2,1)} copy(bf16[1,3,32,32,256]{4,3,2,1,0:T(8,128)(2,1)S(1)} %bitcast.8) | data formatting | bytes 3145728
  (6 shorter events, 0.1 us)
Async XLA Ops:
  89.0 4.5 %copy-start.1 = (bf16[3,1024,256]{2,1,0:T(8,128)(2,1)S(1)}, bf16[3,1024,256]{2,1,0:T(8,128)(2,1)}, u32[]{:S(2)}) copy-start(bf16[3,1024,256]{2,1,0:T(8,128)(2,1)} %get-tuple-element.8) | copy-start | bytes 4718596
  93.4 2.0 %copy-start = (bf16[3,1024,256]{2,1,0:T(8,128)(2,1)S(1)}, bf16[3,1024,256]{2,1,0:T(8,128)(2,1)}, u32[]{:S(2)}) copy-start(bf16[3,1024,256]{2,1,0:T(8,128)(2,1)} %get-tuple-element.9) | copy-start | bytes 4718596

commit v3 on v2

--- a/solution.py
+++ b/solution.py
@@ -18,13 +18,13 @@
 
 
 def kernel(
-    feat_hbm, cot_hbm, w1_hbm, w2_hbm, tab, loc,
-    out, gfeat, gout1, gout2,
-    feat, cot, w1, w2,
+    feat_hbm, cot_hbm, w1_hbm, w2_hbm, near_v, turn_v, near, turn,
+    out_hbm, gfeat_hbm, gout1_hbm, gout2_hbm,
+    feat, cot, w1, w2, out, gfeat, gout1, gout2,
     fa3, c3, d3, wt, pre, dact, xt, grad1, grad2, seams, edges, rimrows, corr, mats, pickrow,
-    edge_out, ag0, ag1, ag2, ag3, pick, got0, got1, got2, got3, tabv, tabs,
+    edge_out, ag0, ag1, ag2, ag3, pick, got0, got1, got2, got3, tab, tabw, tabv, tabs,
     snd, rcore, sx, rx, sy, ry, sz, rz, full,
-    tab_s, tab_r, ag_s, ag_r, pk_s, pk_r, ar_s, ar_r, loc_sem, in_sem,
+    tab_s, tab_r, ag_s, ag_r, pk_s, pk_r, ar_s, ar_r, loc_sem, in_sem, out_sem,
 ):
     ag = (ag0, ag1, ag2, ag3)
     got = (got0, got1, got2, got3)
@@ -36,6 +36,10 @@
     ]
     for copy in loads:
         copy.start()
+    stores = [
+        pltpu.make_async_copy(src, dst, out_sem.at[i])
+        for i, (src, dst) in enumerate(((out, out_hbm), (gfeat, gfeat_hbm), (gout1, gout1_hbm), (gout2, gout2_hbm)))
+    ]
     me = lax.axis_index("tiles")
     xpos = lax.axis_index("members")
     core = lax.rem(me, 2)
@@ -77,8 +81,6 @@
     mats[1] = jnp.where(inside & (m_c == m_t * 32 + 31 - m_j), 1.0, 0.0)
     tile_of = m_t
 
-    pl.semaphore_wait(barrier, 16)
-
     def remote(src, dst, ssem, rsem, target):
         return pltpu.make_async_remote_copy(
             src_ref=src, dst_ref=dst, send_sem=ssem, recv_sem=rsem,
@@ -97,13 +99,17 @@
         make().start()
         sends.append(make)
 
-    for d in range(1, 4):
-        launch(lambda d=d: remote(tab.at[0], tabv.at[ypos * 2 + core], tab_s.at[d - 1], tab_r.at[ypos * 2 + core], tid(zpos, wrap(ypos + d), 0)))
-        launch(lambda d=d: remote(tab.at[1], tabv.at[zpos * 2 + core], tab_s.at[d + 2], tab_r.at[zpos * 2 + core], tid(wrap(zpos + d), ypos, 1)))
-    slot_p = (ypos * core + zpos * (1 - core)) * 2 + core
-    launch(lambda: remote(tab.at[1 - core], tabv.at[slot_p], tab_s.at[6], tab_r.at[slot_p], partner))
-    tab_own = pltpu.make_async_copy(tab.at[core], tabv.at[other * 2 + core], loc_sem.at[0])
-    tab_own.start()
+    def fill_tables():
+        way = turn_v[...]
+        src = 4 * near_v[...] + (way & 3)
+        device = (src * 43691) >> 19
+        z_of, y_of, c_of = device >> 3, (device >> 1) & 3, device & 1
+        row = src - 12 * device
+        for h, at in enumerate((z_of, y_of)):
+            tabw[h] = jnp.zeros((8, 128), jnp.int32)
+            tabw[h, 0:3, 0:4] = (at * 2 + c_of) * 12 + row
+            wide = tabw[h]
+            tab[h] = wide[0:1] + pltpu.roll(wide, 4, 1)[1:2] + pltpu.roll(wide, 8, 1)[2:3]
 
     def dot(a, b):
         return jnp.dot(a, b, preferred_element_type=F32)
@@ -177,15 +183,21 @@
             wait(1, wrap(zpos + d))
         wait(1 - core, zpos * (1 - core) + ypos * core)
 
+    def source(k):
+        way = turn[k // 4, k % 4]
+        device = lax.div(4 * near[k // 4, k % 4] + lax.rem(way, 4), 12)
+        return lax.rem(lax.div(device, 2), 4), lax.div(device, 8), lax.div(way, 4)
+
     def received(n, e):
         rows = []
         for t in range(3):
             k = t * 4 + e
-            rows.append(jnp.concatenate([got[n][0, loc[0, k], k], got[n][1, loc[1, k], k]], axis=1))
+            y_from, z_from, _ = source(k)
+            rows.append(jnp.concatenate([got[n][0, y_from, k], got[n][1, z_from, k]], axis=1))
         return jnp.concatenate(rows, axis=0)
 
     def turned(e, low, high):
-        flip = jnp.where(tile_of == 0, loc[2, e], jnp.where(tile_of == 1, loc[2, 4 + e], loc[2, 8 + e]))[low:high]
+        flip = jnp.where(tile_of == 0, source(e)[2], jnp.where(tile_of == 1, source(4 + e)[2], source(8 + e)[2]))[low:high]
         return jnp.where(flip == 1, mats[1, low:high], mats[0, low:high]).astype(BF16)
 
     def take_seams(n):
@@ -279,7 +291,7 @@
             for b in range(3):
                 wt[a, b * 256:b * 256 + 256, :] = w[2 - a, 2 - b].T
 
-    def grad_inner(g3, dst):
+    def grad_inner(g3, dst, after=()):
         def step(i, carry):
             al = i // 3
             be = i - al * 3
@@ -289,6 +301,8 @@
                 value = part if value is None else value + part
             for h in range(2):
                 dst[h, :, :, 8 - i] = value[:, h * 128:h * 128 + 128].reshape(4, 4, 16, 128)
+            for at, do in after:
+                pl.when(i == at)(do)
             return carry
 
         lax.fori_loop(0, 9, step, 0)
@@ -407,10 +421,21 @@
                 for h in range(2):
                     gouts[g][3 * r + b, :, h * 128:h * 128 + 128] = full[u, h, :, :, b].reshape(256, 128)
 
+    fill_tables()
     loads[0].wait()
     take_edges(lambda t: feat[t].reshape(1024, 256), 0)
     put_edges(0, 0)
+    pl.semaphore_wait(barrier, 16)
     send_edges(0)
+
+    for d in range(1, 4):
+        launch(lambda d=d: remote(tab.at[0], tabv.at[ypos * 2 + core], tab_s.at[d - 1], tab_r.at[ypos * 2 + core], tid(zpos, wrap(ypos + d), 0)))
+        launch(lambda d=d: remote(tab.at[1], tabv.at[zpos * 2 + core], tab_s.at[d + 2], tab_r.at[zpos * 2 + core], tid(wrap(zpos + d), ypos, 1)))
+    slot_p = (ypos * core + zpos * (1 - core)) * 2 + core
+    launch(lambda: remote(tab.at[1 - core], tabv.at[slot_p], tab_s.at[6], tab_r.at[slot_p], partner))
+    tab_own = pltpu.make_async_copy(tab.at[core], tabv.at[other * 2 + core], loc_sem.at[0])
+    tab_own.start()
+
     loads[1].wait()
     loads[2].wait()
     take_edges(lambda t: cot[t].reshape(1024, 256), 1)
@@ -446,12 +471,10 @@
         dact[t, pl.ds(r, ROWS), :] = acc
 
     loads[3].wait()
-    conv3(fa3, lambda a: w1[a].reshape(768, 256), store_pre)
-    forward(0)
+    conv3(fa3, lambda a: w1[a].reshape(768, 256), store_pre, ((4, lambda: forward(0)),))
     each_chunk(load_cot)
     turn_weight(w2)
-    forward(1)
-    conv3(c3, lambda a: wt[a], store_dact)
+    conv3(c3, lambda a: wt[a], store_dact, ((1, lambda: forward(1)),))
     transpose_tiles(fa3)
     turn_weight(w1)
     arrive(0)
@@ -482,36 +505,20 @@
     take_edges(lambda t: d3[t, 32:1056, 256:512], 0)
     rims(0, w1, 3)
     send_edges(3)
-    grad_inner(d3, grad1)
+    grad_inner(d3, grad1, ((3, lambda: forward(2)),))
     grad_seams(0, grad1)
     step_core(0)
-    forward(2)
     transpose_tiles(fa3)
-    step_first(0)
-    grad_inner(c3, grad2)
-    step_second(0)
-    forward(3)
+    grad_inner(c3, grad2, ((1, lambda: step_first(0)), (3, lambda: forward(3))))
     arrive(2)
     take_seams(2)
     grad_seams(1, grad2)
     step_core(1)
-    step_third(0)
-
-    def after_a():
-        step_first(1)
-        step_back_second(0)
-
-    def after_b():
-        step_second(1)
-        step_back_first(0)
-
-    def after_c():
-        step_third(1)
-        step_back_core(0)
-
-    conv3(fa3, lambda a: w2[a].reshape(768, 256), store_pre, ((1, after_a), (4, after_b)))
-    seam_conv(w2, pre)
-    after_c()
+    step_second(0)
+    conv3(
+        fa3, lambda a: w2[a].reshape(768, 256), store_pre,
+        ((1, lambda: step_first(1)), (3, lambda: step_third(0)), (5, lambda: step_second(1))),
+    )
 
     def finish_out(t, r):
         row = pl.multiple_of(r * 128, 128)
@@ -521,26 +528,67 @@
         row = pl.multiple_of(r * 128, 128)
         gfeat[t, pl.ds(row, 128), :] = dact[t, pl.ds(row, 128), :].astype(BF16)
 
+    seam_conv(w2, pre)
+    step_back_second(0)
     each_chunk(finish_out)
-    conv3(d3, lambda a: wt[a], store_dact, ((0, lambda: step_back_second(1)), (2, lambda: step_back_first(1)), (5, lambda: step_back_core(1))))
-    step_end(0)
+    stores[0].start()
+    step_third(1)
+    conv3(
+        d3, lambda a: wt[a], store_dact,
+        ((1, lambda: step_back_first(0)), (3, lambda: step_back_second(1))),
+    )
     arrive(3)
     rim_add(3, dact)
+    step_back_core(0)
+    step_back_first(1)
     each_chunk(finish_gfeat)
+    stores[1].start()
+    step_end(0)
+    stores[2].start()
+    step_back_core(1)
     step_end(1)
+    stores[3].start()
+    for copy in stores:
+        copy.wait()
     for make in sends:
         make().wait_send()
+
+
+def results(factor, out_in, gfeat_in, g1_in, g2_in, out, gfeat, g1, g2, held_g, held, total, sem_in, sem_out):
+    pieces = [(i, g_in, g, 768 * r) for r in range(3) for i, (g_in, g) in enumerate(((g1_in, g1), (g2_in, g2)))]
+    gets = [
+        pltpu.make_async_copy(g_in.at[pl.ds(row, 768)], held_g.at[i, pl.ds(row, 768)], sem_in.at[n])
+        for n, (i, g_in, g, row) in enumerate(pieces)
+    ]
+    puts = [
+        pltpu.make_async_copy(total.at[i, pl.ds(row, 768)], g.at[pl.ds(row, 768)], sem_out.at[n])
+        for n, (i, g_in, g, row) in enumerate(pieces)
+    ]
+    fields = [(i, f_in, f, 1536 * r) for r in range(2) for i, (f_in, f) in enumerate(((out_in, out), (gfeat_in, gfeat)))]
+    gets += [
+        pltpu.make_async_copy(f_in.at[pl.ds(row, 1536)], held.at[i, pl.ds(row, 1536)], sem_in.at[6 + n])
+        for n, (i, f_in, f, row) in enumerate(fields)
+    ]
+    puts += [
+        pltpu.make_async_copy(held.at[i, pl.ds(row, 1536)], f.at[pl.ds(row, 1536)], sem_out.at[6 + n])
+        for n, (i, f_in, f, row) in enumerate(fields)
+    ]
+    for copy in gets:
+        copy.start()
+    for n, (i, g_in, g, row) in enumerate(pieces):
+        gets[n].wait()
+        total[i, pl.ds(row, 768)] = held_g[i, pl.ds(row, 768)].astype(F32) * factor
+        puts[n].start()
+    for n in range(6, 10):
+        gets[n].wait()
+        puts[n].start()
+    for copy in puts:
+        copy.wait()
 
 
 def on_device(features, conv_one, conv_two, cotangent, neighbour_tile, rotation):
     cells_all = lax.axis_size("members") * lax.axis_size("tiles") * 3 * 1024
     factor = 1.0 / math.sqrt(cells_all)
-    source = (4 * neighbour_tile + rotation % 4).reshape(12)
-    device = source // 12
-    z_of, y_of, c_of, row = device // 8, device // 2 % 4, device % 2, source % 12
-    tab = jnp.stack([(z_of * 2 + c_of) * 12 + row, (y_of * 2 + c_of) * 12 + row])
-    tab = jnp.broadcast_to(jnp.pad(tab, ((0, 0), (0, 116)))[:, None], (2, 8, 128))
-    loc = jnp.stack([y_of, z_of, (rotation // 4).reshape(12)])
     vmem = pl.BlockSpec(memory_space=pltpu.VMEM)
     dma = pltpu.SemaphoreType.DMA
     out, gfeat, gout1, gout2 = pl.pallas_call(
@@ -551,13 +599,17 @@
             jax.ShapeDtypeStruct((9, 256, 256), BF16),
             jax.ShapeDtypeStruct((9, 256, 256), BF16),
         ),
-        in_specs=[pl.BlockSpec(memory_space=pl.ANY)] * 4 + [vmem] + [pl.BlockSpec(memory_space=pltpu.SMEM)],
-        out_specs=(vmem,) * 4,
+        in_specs=[pl.BlockSpec(memory_space=pl.ANY)] * 4 + [vmem] * 2 + [pl.BlockSpec(memory_space=pltpu.SMEM)] * 2,
+        out_specs=(pl.BlockSpec(memory_space=pl.ANY),) * 4,
         scratch_shapes=[
             pltpu.VMEM((3, 32, 32, 256), BF16),
             pltpu.VMEM((3, 32, 32, 256), BF16),
             pltpu.VMEM((3, 3, 256, 256), BF16),
             pltpu.VMEM((3, 3, 256, 256), BF16),
+            pltpu.VMEM((3, 1024, 256), BF16),
+            pltpu.VMEM((3, 1024, 256), BF16),
+            pltpu.VMEM((9, 256, 256), BF16),
+            pltpu.VMEM((9, 256, 256), BF16),
             pltpu.VMEM((3, 1088, 768), BF16),
             pltpu.VMEM((3, 1088, 768), BF16),
             pltpu.VMEM((3, 1088, 768), BF16),
@@ -577,8 +629,10 @@
             *[pltpu.VMEM((96, 32, 128), BF16)] * 4,
             pltpu.VMEM((4, 8, 12, 32, 128), BF16),
             *[pltpu.VMEM((2, 4, 12, 32, 128), BF16)] * 4,
-            pltpu.VMEM((8, 8, 128), jnp.int32),
-            pltpu.SMEM((8, 8, 128), jnp.int32),
+            pltpu.VMEM((2, 1, 128), jnp.int32),
+            pltpu.VMEM((2, 8, 128), jnp.int32),
+            pltpu.VMEM((8, 1, 128), jnp.int32),
+            pltpu.SMEM((8, 1, 128), jnp.int32),
             pltpu.VMEM((6, 4, 4, 3, 16, 128), BF16),
             pltpu.VMEM((6, 4, 4, 3, 16, 128), BF16),
             pltpu.VMEM((6, 4, 4, 3, 16, 128), BF16),
@@ -598,17 +652,35 @@
             dma((6, 22)),
             dma((4,)),
             dma((4,)),
+            dma((4,)),
         ],
         compiler_params=pltpu.CompilerParams(
             collective_id=0, has_side_effects=True, vmem_limit_bytes=67043328
         ),
-    )(features[0], cotangent[0], conv_one, conv_two, tab, loc)
-
-    def whole(total):
-        return (total.astype(F32) * factor).reshape(3, 3, 256, 256)
-
+    )(features[0], cotangent[0], conv_one, conv_two, neighbour_tile, rotation, neighbour_tile, rotation)
+
+    anywhere = pl.BlockSpec(memory_space=pl.ANY)
+    out, gfeat, grad1, grad2 = pl.pallas_call(
+        functools.partial(results, factor),
+        in_specs=[anywhere] * 4,
+        out_specs=(anywhere,) * 4,
+        out_shape=(
+            jax.ShapeDtypeStruct((3072, 256), BF16),
+            jax.ShapeDtypeStruct((3072, 256), BF16),
+            jax.ShapeDtypeStruct((2304, 256), F32),
+            jax.ShapeDtypeStruct((2304, 256), F32),
+        ),
+        scratch_shapes=[
+            pltpu.VMEM((2, 2304, 256), BF16),
+            pltpu.VMEM((2, 3072, 256), BF16),
+            pltpu.VMEM((2, 2304, 256), F32),
+            dma((10,)),
+            dma((10,)),
+        ],
+    )(out.reshape(3072, 256), gfeat.reshape(3072, 256), gout1.reshape(2304, 256), gout2.reshape(2304, 256))
     shape = features.shape
-    return (out.reshape(shape), gfeat.reshape(shape), whole(gout1), whole(gout2))
+    kshape = conv_one.shape
+    return (out.reshape(shape), gfeat.reshape(shape), grad1.reshape(kshape), grad2.reshape(kshape))
 
 
 def solution(mesh):

time: 96.8 us -> 87.7 us (0.906)
  other arithmetic: 5.84 us -> 0 us
  local copies, waits for them, and re-layouts: 4.06 us -> 0 us
  Pallas kernels: 86 us -> 87 us
    pallas_call x0 -> x1, Pallas kernels: none -> 5.06 us  [on_device(): pl.pallas_call(functools.partial(results, factor), in_specs=[anywhere] *...]
    mul x1 -> x0, other arithmetic: 4.47 us -> none  [whole(): return (total.astype(F32) * factor).reshape(3, 3, 256, 256)]
    pallas_call x1, Pallas kernels: 86 us -> 81.9 us  [on_device(): pl.pallas_call(kernel, out_shape=(jax.ShapeDtypeStruct((3, 1024, 256), BF...]
    unnamed x6 -> x0, local copies, waits for them, and re-layouts: 3.12 us -> none
where the time goes in v3:
time: 87.7 us; the launch traced here: 87.6 us
  Pallas kernels  87 us (99%)
    pallas_call x1, Pallas kernels, on_device(): pl.pallas_call(kernel, out_shape=(jax.ShapeDtypeStruct((3, 1024, 256), BF...  81.9 us
    pallas_call x1, Pallas kernels, on_device(): pl.pallas_call(functools.partial(results, factor), in_specs=[anywhere] *...  5.06 us

profile of v3, /device:TPU:1, one launch (start us, length us, event | category | flops | bytes accessed | tf_op | source)
XLA Modules:
  0.0 87.6 jit_solution(5594077477787820143)
XLA Ops:
  0.6 81.9 %shard_map.93 = (bf16[3,1024,256]{2,1,0:T(8,128)(2,1)}, bf16[3,1024,256]{2,1,0:T(8,128)(2,1)}, bf16[9,256,256]{2,1,0:T(8,128)(2,1)}, bf16[9,256,256]{2,1,0:T(8,128)(2,1)}) custom-call(bf16[3,32,32,256]{3,2,1,0:T(8,128)(2,1)} %bitcast.10, bf16[3,32,32,256]{3,2,1,0:T(8,128)(2,1)} %bitcast.11, bf16[3,3,256,256]{3,2,1,0:T(8,128)(2,1)} %w1_hbm.1, ...), custom_call_target="tpu_custom_call" | custom-call | tf_op jit(solution)/shard_map/pallas_call | solution.py:594
  82.5 5.1 %shard_map.94 = (bf16[3072,256]{1,0:T(8,128)(2,1)}, bf16[3072,256]{1,0:T(8,128)(2,1)}, f32[2304,256]{1,0:T(8,128)}, f32[2304,256]{1,0:T(8,128)}) custom-call(bf16[3072,256]{1,0:T(8,128)(2,1)} %bitcast.12, bf16[3072,256]{1,0:T(8,128)(2,1)} %bitcast.13, bf16[2304,256]{1,0:T(8,128)(2,1)} %bitcast.14, bf16[2304,256]{1,0:T(8,128)(2,1)} %bitcast.15), custom_call_target="tpu_custom_call" | custom-call | tf_op jit(solution)/shard_map/pallas_call | solution.py:663

commit v4 on v3

--- a/solution.py
+++ b/solution.py
@@ -11,7 +11,7 @@
 MESH = pl.DeviceIdType.MESH
 F32 = jnp.float32
 BF16 = jnp.bfloat16
-ROWS = 512
+ROWS = 1024
 
 
 ORDER = ("xyz", "yzx", "zxy")
@@ -471,10 +471,10 @@
         dact[t, pl.ds(r, ROWS), :] = acc
 
     loads[3].wait()
-    conv3(fa3, lambda a: w1[a].reshape(768, 256), store_pre, ((4, lambda: forward(0)),))
+    conv3(fa3, lambda a: w1[a].reshape(768, 256), store_pre, ((2, lambda: forward(0)),))
     each_chunk(load_cot)
     turn_weight(w2)
-    conv3(c3, lambda a: wt[a], store_dact, ((1, lambda: forward(1)),))
+    conv3(c3, lambda a: wt[a], store_dact, ((0, lambda: forward(1)),))
     transpose_tiles(fa3)
     turn_weight(w1)
     arrive(0)
@@ -517,7 +517,7 @@
     step_second(0)
     conv3(
         fa3, lambda a: w2[a].reshape(768, 256), store_pre,
-        ((1, lambda: step_first(1)), (3, lambda: step_third(0)), (5, lambda: step_second(1))),
+        ((0, lambda: step_first(1)), (1, lambda: step_third(0)), (2, lambda: step_second(1))),
     )
 
     def finish_out(t, r):
@@ -535,7 +535,7 @@
     step_third(1)
     conv3(
         d3, lambda a: wt[a], store_dact,
-        ((1, lambda: step_back_first(0)), (3, lambda: step_back_second(1))),
+        ((0, lambda: step_back_first(0)), (1, lambda: step_back_second(1))),
     )
     arrive(3)
     rim_add(3, dact)

time: 87.7 us -> 87.1 us (level)
  no operation moved by 1% of the time
where the time goes in v4:
time: 87.1 us; the launch traced here: 87 us
  Pallas kernels  86.2 us (99%)
    pallas_call x1, Pallas kernels, on_device(): pl.pallas_call(kernel, out_shape=(jax.ShapeDtypeStruct((3, 1024, 256), BF...  81.1 us
    pallas_call x1, Pallas kernels, on_device(): pl.pallas_call(functools.partial(results, factor), in_specs=[anywhere] *...  5.06 us

profile of v4, /device:TPU:1, one launch (start us, length us, event | category | flops | bytes accessed | tf_op | source)
XLA Modules:
  0.0 87.0 jit_solution(12576579561857720952)
XLA Ops:
  0.6 81.1 %shard_map.93 = (bf16[3,1024,256]{2,1,0:T(8,128)(2,1)}, bf16[3,1024,256]{2,1,0:T(8,128)(2,1)}, bf16[9,256,256]{2,1,0:T(8,128)(2,1)}, bf16[9,256,256]{2,1,0:T(8,128)(2,1)}) custom-call(bf16[3,32,32,256]{3,2,1,0:T(8,128)(2,1)} %bitcast.10, bf16[3,32,32,256]{3,2,1,0:T(8,128)(2,1)} %bitcast.11, bf16[3,3,256,256]{3,2,1,0:T(8,128)(2,1)} %w1_hbm.1, ...), custom_call_target="tpu_custom_call" | custom-call | tf_op jit(solution)/shard_map/pallas_call | solution.py:594
  81.7 5.1 %shard_map.94 = (bf16[3072,256]{1,0:T(8,128)(2,1)}, bf16[3072,256]{1,0:T(8,128)(2,1)}, f32[2304,256]{1,0:T(8,128)}, f32[2304,256]{1,0:T(8,128)}) custom-call(bf16[3072,256]{1,0:T(8,128)(2,1)} %bitcast.12, bf16[3072,256]{1,0:T(8,128)(2,1)} %bitcast.13, bf16[2304,256]{1,0:T(8,128)(2,1)} %bitcast.14, bf16[2304,256]{1,0:T(8,128)(2,1)} %bitcast.15), custom_call_target="tpu_custom_call" | custom-call | tf_op jit(solution)/shard_map/pallas_call | solution.py:663
